TPU v7x, 32 devices: a whole 2x2x4 slice. The times are simulated.
32 devices in a mesh: dp: 8 (over z, x), ctx: 4 (over y, core).
Axes of the slice: x: 2, y: 2, z: 4, core: 2. Of those that a mesh axis runs over, the one named last changes fastest.
Arguments:
- features: bfloat16 [4096, 4096], P(('dp', 'ctx')), may hold values from -6 to 6
- gate_in: bfloat16 [4096, 4096], P(('dp', 'ctx')), may hold values from -6 to 6
- gate_out: bfloat16 [4096, 4096], P(('dp', 'ctx')), may hold values from -6 to 6
- value_weight: bfloat16 [4096, 4096], P('dp', 'ctx'), may hold values from -0.09375 to 0.09375
- short_taps: float32 [3, 7, 4096], replicated, may hold values from -2 to 2
- medium_taps: bfloat16 [128, 256], replicated, may hold values from -0.5 to 0.5
- cotangent: bfloat16 [4096, 4096], P(('dp', 'ctx')), may hold values from -6 to 6
Outputs:
- layer_out: bfloat16 [4096, 4096], P(('dp', 'ctx'))
- grad_features: bfloat16 [4096, 4096], P(('dp', 'ctx'))
- grad_gate_in: bfloat16 [4096, 4096], P(('dp', 'ctx'))
- grad_gate_out: bfloat16 [4096, 4096], P(('dp', 'ctx'))
- grad_weight: bfloat16 [4096, 4096], P('dp', 'ctx')
- grad_short: float32 [3, 7, 4096], P(None, None, 'ctx')
- grad_medium: float32 [128, 256], P(None, 'ctx')
All inputs are finite; a program needn't handle non-finite values.
Results may differ from a plain program's by a relative error of at most 0.025.
Values may be sent and summed in bfloat16 or wider, within the bound.
A program may use at most 256 MiB of HBM per device.

v0:
```python
import math

import jax
import jax.numpy as jnp
from jax import lax
from jax.sharding import PartitionSpec as P


def causal_conv(stream, conv_taps, prior_rows):
    conv_edge = conv_taps.shape[0] - 1
    row_count = stream.shape[0]
    extended = jnp.concatenate([prior_rows, stream], axis=0)
    running = conv_taps[0] * extended[conv_edge : conv_edge + row_count]
    for shift_back in range(1, conv_edge + 1):
        running = (
            running
            + conv_taps[shift_back]
            * extended[conv_edge - shift_back : conv_edge - shift_back + row_count]
        )
    return running


def conv_back(gradient, conv_taps, later_rows):
    conv_edge = conv_taps.shape[0] - 1
    row_count = gradient.shape[0]
    extended = jnp.concatenate([gradient, later_rows], axis=0)
    running = conv_taps[0] * extended[:row_count]
    for ahead in range(1, conv_edge + 1):
        running = running + conv_taps[ahead] * extended[ahead : ahead + row_count]
    return running


def conv_taps_grad(gradient, stream, prior_rows):
    conv_edge = prior_rows.shape[0]
    row_count = stream.shape[0]
    extended = jnp.concatenate([prior_rows, stream], axis=0)
    return jnp.stack(
        [
            jnp.sum(
                gradient * extended[conv_edge - shift_back : conv_edge - shift_back + row_count],
                axis=0,
            )
            for shift_back in range(conv_edge + 1)
        ]
    )


def toeplitz_table(medium):
    filter_span, group_count = medium.shape
    padded = jnp.concatenate(
        [
            jnp.zeros((1, group_count), medium.dtype),
            medium[::-1],
            jnp.zeros((filter_span, group_count), medium.dtype),
        ],
        axis=0,
    )
    tiled = jnp.tile(padded.T, (1, filter_span))
    return tiled[:, : 2 * filter_span * filter_span].reshape(
        group_count, filter_span, 2 * filter_span
    )


def fold_table(grad_table):
    group_count, filter_span, double_span = grad_table.shape
    flat = grad_table.reshape(group_count, filter_span * double_span)
    flat = jnp.concatenate([flat, jnp.zeros((group_count, filter_span), grad_table.dtype)], axis=1)
    summed = jnp.sum(flat.reshape(group_count, filter_span, double_span + 1), axis=1)
    return summed[:, 1 : filter_span + 1][:, ::-1].T


def apply_toeplitz(toeplitz, before, product):
    group_count, filter_span = (toeplitz.shape[0], toeplitz.shape[1])
    row_count, channels = product.shape
    block_shape = (row_count // filter_span, filter_span, group_count, channels // group_count)
    extended = jnp.concatenate([before, product], axis=0)
    lower_half = extended[:row_count].reshape(block_shape)
    upper_half = extended[filter_span:].reshape(block_shape)
    window = jnp.concatenate([lower_half, upper_half], axis=1)
    filtered = jnp.einsum("gij,bjgs->bigs", toeplitz, window, preferred_element_type=jnp.float32)
    return (filtered.reshape(row_count, channels), window)


def toeplitz_back(toeplitz, grad_filtered, later_rows, window):
    group_count, filter_span = (toeplitz.shape[0], toeplitz.shape[1])
    row_count, channels = grad_filtered.shape
    block_shape = (row_count // filter_span, filter_span, group_count, channels // group_count)
    current = grad_filtered.reshape(block_shape)
    following = jnp.concatenate([grad_filtered[filter_span:], later_rows], axis=0).reshape(
        block_shape
    )
    grad_product = jnp.einsum(
        "gij,bigs->bjgs", toeplitz[:, :, filter_span:], current, preferred_element_type=jnp.float32
    )
    grad_product = grad_product + jnp.einsum(
        "gij,bigs->bjgs",
        toeplitz[:, :, :filter_span],
        following,
        preferred_element_type=jnp.float32,
    )
    grad_table = jnp.einsum("bigs,bjgs->gij", current, window, preferred_element_type=jnp.float32)
    return (grad_product.reshape(row_count, channels), fold_table(grad_table))


def mixer_pass(
    stream_in,
    stream_out,
    stream_values,
    cot_rows,
    conv_taps,
    medium,
    fetch_rims,
    fetch_before,
    fetch_after,
    fetch_later,
):
    row_count = stream_in.shape[0]
    filter_span = medium.shape[0]
    conv_edge = conv_taps.shape[1] - 1
    streams = (stream_in, stream_out, stream_values)
    rims = fetch_rims(tuple((stream[row_count - conv_edge :] for stream in streams)))
    convs = [causal_conv(streams[index], conv_taps[index], rims[index]) for index in range(3)]
    product = (convs[0] * convs[2]).astype(jnp.bfloat16)
    toeplitz = toeplitz_table(medium)
    filtered, window = apply_toeplitz(
        toeplitz, fetch_before(product[row_count - filter_span :]), product
    )
    layer_out = (convs[1] * filtered).astype(jnp.bfloat16)
    grad_filtered = (cot_rows * convs[1]).astype(jnp.bfloat16)
    grad_product, medium_grad = toeplitz_back(
        toeplitz, grad_filtered, fetch_after(grad_filtered[:filter_span]), window
    )
    grad_convs = (grad_product * convs[2], cot_rows * filtered, grad_product * convs[0])
    later = fetch_later(tuple((gradient[:conv_edge] for gradient in grad_convs)))
    grad_streams = [
        conv_back(grad_convs[index], conv_taps[index], later[index]) for index in range(3)
    ]
    short_grad = jnp.stack(
        [conv_taps_grad(grad_convs[index], streams[index], rims[index]) for index in range(3)]
    )
    return (layer_out, grad_streams, short_grad, medium_grad)


def zero_tuple(tail_rows):
    return tuple((jnp.zeros_like(piece) for piece in tail_rows))


def local(features, gate_in, gate_out, value_weight, short_taps, medium_taps, cotangent):
    ctx_count = lax.axis_size("ctx")
    dp_count = lax.axis_size("dp")
    ctx_index = lax.axis_index("ctx")
    own_rows, channels = features.shape
    block_cols = value_weight.shape[1]
    group_count = medium_taps.shape[1]
    total_rows = own_rows * ctx_count * dp_count
    row_scale = 1.0 / math.sqrt(total_rows)
    group_scale = 1.0 / math.sqrt(total_rows * (channels // group_count))
    weight_block = lax.all_gather(value_weight, "dp", axis=0, tiled=True)
    feature_window = lax.all_gather(features, "ctx", axis=0, tiled=True)
    values_block = jnp.dot(feature_window, weight_block, preferred_element_type=jnp.float32).astype(
        jnp.bfloat16
    )
    block_in, block_out, block_cot = (
        lax.all_to_all(gate_in, "ctx", split_axis=1, concat_axis=0, tiled=True),
        lax.all_to_all(gate_out, "ctx", split_axis=1, concat_axis=0, tiled=True),
        lax.all_to_all(cotangent, "ctx", split_axis=1, concat_axis=0, tiled=True),
    )
    taps_block = lax.dynamic_slice_in_dim(short_taps, ctx_index * block_cols, block_cols, 2)
    group_block = group_count // ctx_count
    medium_block = lax.dynamic_slice_in_dim(medium_taps, ctx_index * group_block, group_block, 1)
    out_block, grad_streams, short_grad, medium_grad = mixer_pass(
        block_in,
        block_out,
        values_block,
        block_cot,
        taps_block,
        medium_block,
        zero_tuple,
        jnp.zeros_like,
        jnp.zeros_like,
        zero_tuple,
    )
    layer_out = lax.all_to_all(out_block, "ctx", split_axis=0, concat_axis=1, tiled=True)
    grad_gate_in, grad_gate_out = (
        lax.all_to_all(
            grad_streams[0].astype(jnp.bfloat16), "ctx", split_axis=0, concat_axis=1, tiled=True
        ),
        lax.all_to_all(
            grad_streams[1].astype(jnp.bfloat16), "ctx", split_axis=0, concat_axis=1, tiled=True
        ),
    )
    grad_values = grad_streams[2].astype(jnp.bfloat16)
    grad_short, grad_medium = (
        lax.psum((short_grad * row_scale).astype(jnp.bfloat16), "dp").astype(jnp.float32),
        lax.psum((medium_grad * group_scale).astype(jnp.bfloat16), "dp").astype(jnp.float32),
    )
    grad_weight = lax.psum_scatter(
        (
            lax.dot_general(
                feature_window,
                grad_values,
                (((0,), (0,)), ((), ())),
                preferred_element_type=jnp.float32,
            )
            * row_scale
        ).astype(jnp.bfloat16),
        "dp",
        scatter_dimension=0,
        tiled=True,
    )
    grad_features = lax.psum_scatter(
        lax.dot_general(
            grad_values, weight_block, (((1,), (1,)), ((), ())), preferred_element_type=jnp.float32
        ).astype(jnp.bfloat16),
        "ctx",
        scatter_dimension=0,
        tiled=True,
    )
    return (
        layer_out,
        grad_features,
        grad_gate_in,
        grad_gate_out,
        grad_weight,
        grad_short,
        grad_medium,
    )


def solution(mesh):
    in_specs = (
        P(("dp", "ctx"), None),
        P(("dp", "ctx"), None),
        P(("dp", "ctx"), None),
        P("dp", "ctx"),
        P(),
        P(),
        P(("dp", "ctx"), None),
    )
    out_specs = (
        P(("dp", "ctx"), None),
        P(("dp", "ctx"), None),
        P(("dp", "ctx"), None),
        P(("dp", "ctx"), None),
        P("dp", "ctx"),
        P(None, None, "ctx"),
        P(None, "ctx"),
    )
    return jax.shard_map(local, mesh=mesh, in_specs=in_specs, out_specs=out_specs, check_vma=False)
```

profile of v0, /device:TPU:0, one launch (start us, length us, event | category | flops | bytes accessed | tf_op | source)
XLA Modules:
  0.0 426.1 jit_solution(8969090850510553351)
XLA Ops:
  10.0 4.2 all-to-all-start
  15.5 19.7 %all-to-all-done = bf16[128,4,1024]{0,2,1:T(8,128)(2,1)S(1)} async-done(((bf16[128,4,1024]{0,2,1:T(8,128)(2,1)}), bf16[128,4,1024]{0,2,1:T(8,128)(2,1)S(1)}, u32[]{:S(2)}, u32[]{:S(2)}) %all-to-all-start) | async-done | bytes 1048608 | tf_op jit(solution)/shard_map/all_to_all | solution.py:165
  35.3 3.5 all-to-all-start.3
  42.5 10.9 %tile.10 = bf16[64,32896]{1,0:T(8,128)(2,1)} reshape(bf16[64,128,257]{2,1,0:T(8,128)(2,1)} %tile.4) | data formatting | bytes 8421376 | tf_op jit(solution)/shard_map/tile | solution.py:58
  62.6 3.5 all-to-all-start.1
  70.5 6.7 %fusion.43 = (bf16[512,1024]{1,0:T(8,128)(2,1)S(1)}, f32[512,1024]{1,0:T(8,128)}) fusion(f32[4,128,1024]{2,1,0:T(8,128)S(1)} %copy.56, f32[1024]{0:T(1024)S(1)} %bitcast.192, f32[1024]{0:T(1024)S(1)} %bitcast.194, f32[1024]{0:T(1024)S(1)} %bitcast.196, f32[1024]{0:T(1024)S(1)} %bitcast.198, f32[1024]{0:T(1024)S(1)} %bitcast.200, ...), kind=kLoop, calls=%fused_computation.91 | loop fusion | flops 11534336 | bytes 6320128 | tf_op jit(solution)/shard_map/convert_element_type | solution.py:129
  91.1 98.0 %all-gather.5.cloned.1.call-done = bf16[4096,1024]{1,0:T(8,128)(2,1)} async-done(((bf16[512,1024]{1,0:T(8,128)(2,1)}), bf16[4096,1024]{1,0:T(8,128)(2,1)}) %all-gather.5.cloned.1.call-update) | async-done | bytes 8388624 | tf_op jit(solution)/shard_map/all_gather | solution.py:158
  189.1 10.1 %convolution_convert_fusion.1 = bf16[512,1024]{1,0:T(8,128)(2,1)} fusion(bf16[512,4096]{1,0:T(8,128)(2,1)} %all-gather.3.cloned.1.call-done, bf16[4096,1024]{1,0:T(8,128)(2,1)} %all-gather.5.cloned.1.call-done), kind=kOutput, calls=%fused_computation.102 | convolution fusion | flops 4295491584 | bytes 13631488 | tf_op jit(solution)/shard_map/dot_general | solution.py:160
  199.3 8.8 %fusion.27 = (f32[1024]{0:T(1024)S(1)}, f32[1024]{0:T(1024)S(1)}, f32[1024]{0:T(1024)S(1)}, f32[1024]{0:T(1024)S(1)}, f32[1024]{0:T(1024)S(1)}, /*index=5*/f32[1...) fusion(bf16[512,1024]{1,0:T(8,128)(2,1)S(1)} %bitcast.157, ...), kind=kLoop, calls=%fused_computation.69 | loop fusion | flops 22012928 | bytes 9494528 | tf_op jit(solution)/shard_map/reduce_sum | solution.py:39
  208.1 7.0 %fusion.40 = (f32[1024]{0:T(1024)S(1)}, f32[1024]{0:T(1024)S(1)}, f32[1024]{0:T(1024)S(1)}, f32[1024]{0:T(1024)S(1)}, f32[1024]{0:T(1024)S(1)}, /*index=5*/f32[1...) fusion(bf16[512,1024]{1,0:T(8,128)(2,1)S(1)} %copy-done.17, ...), kind=kLoop, calls=%fused_computation.82 | loop fusion | flops 29352960 | bytes 11591680 | tf_op jit(solution)/shard_map/reduce_sum | solution.py:39
  216.8 6.8 %fusion = bf16[4096,1024]{0,1:T(8,128)(2,1)} fusion(bf16[512,1024]{1,0:T(8,128)(2,1)S(1)} %add_convert_fusion.2, bf16[512,4096]{1,0:T(8,128)(2,1)S(1)} %copy-done.21), kind=kOutput, calls=%fused_computation.1 | convolution fusion | flops 4303355904 | bytes 13631488 | tf_op jit(solution)/shard_map/dot_general | solution.py:199
  223.7 9.5 %convolution_convert_fusion = bf16[512,4096]{1,0:T(8,128)(2,1)} fusion(bf16[512,1024]{1,0:T(8,128)(2,1)S(1)} %add_convert_fusion.2, bf16[4096,1024]{1,0:T(8,128)(2,1)} %all-gather.5.cloned.1.call-done), kind=kOutput, calls=%fused_computation.2 | convolution fusion | flops 4297064448 | bytes 13631488 | tf_op jit(solution)/shard_map/dot_general | solution.py:212
  252.7 4.6 %fusion.14 = (f32[1024]{0:T(1024)S(1)}, f32[1024]{0:T(1024)S(1)}, f32[1024]{0:T(1024)S(1)}, f32[1024]{0:T(1024)S(1)}, f32[1024]{0:T(1024)S(1)}, /*index=5*/f32[1...) fusion(bf16[512,1024]{1,0:T(8,128)(2,1)S(1)} %bitcast.160, f32[512,1024]{1,0:T(8,128)} %copy.53, ...), kind=kLoop, calls=%fused_computation.56 | loop fusion | flops 11003904 | bytes 10510336 | tf_op jit(solution)/shard_map/reduce_sum | solution.py:39
  257.3 17.6 %all_to_all.108 = bf16[4,128,1024]{2,1,0:T(8,128)(2,1)} all-to-all(bf16[4,128,1024]{2,1,0:T(8,128)(2,1)S(1)} %bitcast.167), channel_id=1, replica_groups=mesh['dp'=8,'ctx'=4] {'ctx'}, dimensions={0} | all-to-all | bytes 2097152 | tf_op jit(solution)/shard_map/all_to_all | solution.py:183
  274.9 4.3 all-to-all-start.4
  279.2 8.3 %add_convert_fusion = bf16[512,1024]{1,0:T(8,128)(2,1)} fusion(f32[512,1024]{1,0:T(8,128)} %get-tuple-element.52, f32[1024]{0:T(1024)S(1)} %bitcast.193, f32[1024]{0:T(1024)S(1)} %bitcast.195, f32[1024]{0:T(1024)S(1)} %bitcast.197, f32[1024]{0:T(1024)S(1)} %bitcast.199, f32[1024]{0:T(1024)S(1)} %bitcast.201, f32[1024]{0:T(1024)S(1)} %bitcast.203, ...), kind=kLoop, calls=%fused_computation.95 | loop fusion | flops 7340032 | bytes 3174400 | tf_op jit(solution)/shard_map/convert_element_type | solution.py:189
  287.6 6.1 %all-to-all-done.4 = bf16[4,128,1024]{2,1,0:T(8,128)(2,1)} async-done(((bf16[4,128,1024]{2,1,0:T(8,128)(2,1)}), bf16[4,128,1024]{2,1,0:T(8,128)(2,1)}, u32[]{:S(2)}, u32[]{:S(2)}) %all-to-all-start.4) | async-done | bytes 1048608 | tf_op jit(solution)/shard_map/all_to_all | solution.py:185
  293.7 4.4 %all-to-all-start.5 = ((bf16[4,128,1024]{2,1,0:T(8,128)(2,1)}), bf16[4,128,1024]{2,1,0:T(8,128)(2,1)}, u32[]{:S(2)}, u32[]{:S(2)}) async-start(bf16[4,128,1024]{2,1,0:T(8,128)(2,1)} %bitcast.170), calls=%async_computation.6 | async-start | bytes 2097152 | tf_op jit(solution)/shard_map/all_to_all | solution.py:188
  299.4 4.7 %copy.84 = f32[8,8,128,256]{3,1,2,0:T(8,128)S(1)} copy(f32[8,8,128,256]{3,2,1,0:T(8,128)S(1)} %bitcast.155) | data formatting | bytes 16777216
  304.2 3.9 concatenate.46
  308.1 14.3 %reshape.123 = f32[64,128,257]{2,1,0:T(8,128)} reshape(f32[64,32896]{1,0:T(8,128)} %concatenate.46) | data formatting | bytes 16842752 | tf_op jit(solution)/shard_map/reshape | solution.py:68
  322.4 6.3 %reduce_sum.219 = f32[64,257]{1,0:T(8,128)S(1)} reduce(f32[64,128,257]{2,1,0:T(8,128)} %reshape.123, f32[]{:T(128)} %constant.1.clone.1), dimensions={1}, to_apply=%region_24.0 | reduce | flops 2088896 | bytes 8487172 | tf_op jit(solution)/shard_map/reduce_sum | solution.py:68
  329.1 36.9 %all-reduce.9 = (bf16[3,7,1024]{2,1,0:T(8,128)(2,1)S(1)}, bf16[128,64]{0,1:T(8,128)(2,1)S(1)}) all-reduce(bf16[3,7,1024]{2,1,0:T(8,128)(2,1)S(1)} %fusion.52, bf16[128,64]{0,1:T(8,128)(2,1)S(1)} %fusion.53), channel_id=1, replica_groups=mesh['dp'=8,'ctx'=4] {'dp'}, use_global_device_ids=true, to_apply=%region_23.0 | all-reduce | flops 29696 | bytes 118784 | tf_op jit(solution)/shard_map/psum | solution.py:194
  376.7 42.6 %reduce-scatter.3.cloned.1.call-done = bf16[128,4096]{1,0:T(8,128)(2,1)} async-done(((bf16[512,4096]{1,0:T(8,128)(2,1)}), bf16[128,4096]{1,0:T(8,128)(2,1)}) %reduce-scatter.3.cloned.1.call-update) | async-done | bytes 1048592 | tf_op jit(solution)/shard_map/reduce_scatter | solution.py:211
  (116 shorter events, 68.9 us)
Async XLA Ops:
  7.2 31.6 %copy-start = (bf16[128,256]{1,0:T(8,128)(2,1)S(1)}, bf16[128,256]{1,0:T(8,128)(2,1)}, u32[]{:S(2)}) copy-start(bf16[128,256]{1,0:T(8,128)(2,1)} %param.12) | copy-start | bytes 196612
  7.2 83.9 %all-gather.3.cloned.1.call-start = ((), (), s32[]{:S(2)}) async-start(), calls=%async_computation.8 | async-start | bytes 5242880 | tf_op jit(solution)/shard_map/all_gather | solution.py:159
  7.9 181.2 %all-gather.5.cloned.1.call-start = ((), (), s32[]{:S(2)}) async-start(), calls=%async_computation.9 | async-start | bytes 9437184 | tf_op jit(solution)/shard_map/all_gather | solution.py:158
  8.7 5.6 %copy-start.19 = (bf16[128,4096]{1,0:T(8,128)(2,1)S(1)}, bf16[128,4096]{1,0:T(8,128)(2,1)}, u32[]{:S(2)}) copy-start(bf16[128,4096]{1,0:T(8,128)(2,1)} %param.13) | copy-start | bytes 3145732
  10.0 25.3 %all-to-all-start = ((bf16[128,4,1024]{0,2,1:T(8,128)(2,1)}), bf16[128,4,1024]{0,2,1:T(8,128)(2,1)S(1)}, u32[]{:S(2)}, u32[]{:S(2)}) async-start(bf16[128,4,1024]{0,2,1:T(8,128)(2,1)} %bitcast.1), calls=%async_computation | async-start | bytes 2097152 | tf_op jit(solution)/shard_map/all_to_all | solution.py:165
  35.3 26.0 %copy-start.11 = (bf16[128,4,1024]{0,2,1:T(8,128)(2,1)}, bf16[128,4,1024]{0,2,1:T(8,128)(2,1)S(1)}, u32[]{:S(2)}) copy-start(bf16[128,4,1024]{0,2,1:T(8,128)(2,1)S(1)} %all-to-all-done) | copy-start | bytes 3145732
  35.3 27.4 %all-to-all-start.3 = ((bf16[128,4,1024]{0,2,1:T(8,128)(2,1)}), bf16[128,4,1024]{0,2,1:T(8,128)(2,1)S(1)}, u32[]{:S(2)}, u32[]{:S(2)}) async-start(bf16[128,4,1024]{0,2,1:T(8,128)(2,1)} %bitcast.33), calls=%async_computation.3 | async-start | bytes 2097152 | tf_op jit(solution)/shard_map/all_to_all | solution.py:166
  62.6 136.6 %all-to-all-start.1 = ((bf16[128,4,1024]{2,0,1:T(8,128)(2,1)}), bf16[128,4,1024]{2,0,1:T(8,128)(2,1)S(1)}, u32[]{:S(2)}, u32[]{:S(2)}) async-start(bf16[128,4,1024]{2,0,1:T(8,128)(2,1)} %bitcast.169), calls=%async_computation.1 | async-start | bytes 2097152 | tf_op jit(solution)/shard_map/all_to_all | solution.py:164
  66.2 308.3 %reduce-scatter.5.cloned.1.call-start = ((), (), s32[]{:S(2)}) async-start(), calls=%async_computation.11 | async-start | bytes 9437184 | tf_op jit(solution)/shard_map/reduce_scatter | solution.py:197
  70.5 6.8 %copy-start.4 = (f32[4,128,1024]{2,1,0:T(8,128)}, f32[4,128,1024]{2,1,0:T(8,128)S(1)}, u32[]{:S(2)}) copy-start(f32[4,128,1024]{2,1,0:T(8,128)S(1)} %copy.56) | copy-start | bytes 6291460
  82.7 3.2 copy-start.2
  199.3 8.8 %copy-start.17 = (bf16[512,1024]{1,0:T(8,128)(2,1)S(1)}, bf16[512,1024]{1,0:T(8,128)(2,1)}, u32[]{:S(2)}) copy-start(bf16[512,1024]{1,0:T(8,128)(2,1)} %convolution_convert_fusion.1) | copy-start | bytes 3145732
  208.1 8.7 %copy-start.21 = (bf16[512,4096]{1,0:T(8,128)(2,1)S(1)}, bf16[512,4096]{1,0:T(8,128)(2,1)}, u32[]{:S(2)}) copy-start(bf16[512,4096]{1,0:T(8,128)(2,1)} %all-gather.3.cloned.1.call-done) | copy-start | bytes 12582916
  223.7 195.7 %reduce-scatter.3.cloned.1.call-start = ((), (), s32[]{:S(2)}) async-start(), calls=%async_computation.10 | async-start | bytes 5242880 | tf_op jit(solution)/shard_map/reduce_scatter | solution.py:211
  238.6 6.7 %copy-start.14 = (f32[128,4,1024]{0,2,1:T(8,128)S(1)}, f32[128,4,1024]{0,2,1:T(8,128)}, u32[]{:S(2)}) copy-start(f32[128,4,1024]{0,2,1:T(8,128)} %get-tuple-element.58) | copy-start | bytes 6291460
  239.7 5.6 %copy-start.12 = (bf16[128,4,1024]{0,2,1:T(8,128)(2,1)S(1)}, bf16[128,4,1024]{0,2,1:T(8,128)(2,1)}, u32[]{:S(2)}) copy-start(bf16[128,4,1024]{0,2,1:T(8,128)(2,1)} %copy-done.11) | copy-start | bytes 3145732
  242.0 3.4 copy-start.3
  249.6 3.1 copy-start.8
  274.9 18.8 %all-to-all-start.4 = ((bf16[4,128,1024]{2,1,0:T(8,128)(2,1)}), bf16[4,128,1024]{2,1,0:T(8,128)(2,1)}, u32[]{:S(2)}, u32[]{:S(2)}) async-start(bf16[4,128,1024]{2,1,0:T(8,128)(2,1)} %bitcast.41), calls=%async_computation.5 | async-start | bytes 2097152 | tf_op jit(solution)/shard_map/all_to_all | solution.py:185
  279.2 18.9 %copy-start.7 = (bf16[4,256,64,16]{1,3,0,2:T(8,128)(2,1)S(1)}, bf16[4,256,64,16]{1,3,0,2:T(8,128)(2,1)}, u32[]{:S(2)}) copy-start(bf16[4,256,64,16]{1,3,0,2:T(8,128)(2,1)} %copy-done.6) | copy-start | bytes 6291460
  279.2 18.9 %copy-start.10 = (bf16[4,128,64,16]{1,0,3,2:T(4,128)(2,1)S(1)}, bf16[4,128,64,16]{1,0,3,2:T(4,128)(2,1)}, u32[]{:S(2)}) copy-start(bf16[4,128,64,16]{1,0,3,2:T(4,128)(2,1)} %copy-done.9) | copy-start | bytes 3145732
  293.7 77.8 %all-to-all-start.5 = ((bf16[4,128,1024]{2,1,0:T(8,128)(2,1)}), bf16[4,128,1024]{2,1,0:T(8,128)(2,1)}, u32[]{:S(2)}, u32[]{:S(2)}) async-start(bf16[4,128,1024]{2,1,0:T(8,128)(2,1)} %bitcast.170), calls=%async_computation.6 | async-start | bytes 2097152 | tf_op jit(solution)/shard_map/all_to_all | solution.py:188
  322.4 44.9 %copy-start.16 = (bf16[4,128,1024]{2,1,0:T(8,128)(2,1)S(1)}, bf16[4,128,1024]{2,1,0:T(8,128)(2,1)}, u32[]{:S(2)}) copy-start(bf16[4,128,1024]{2,1,0:T(8,128)(2,1)} %all_to_all.108) | copy-start | bytes 3145732
  373.1 46.2 %copy-start.1 = (bf16[128,256]{1,0:T(8,128)(2,1)S(1)}, bf16[128,256]{1,0:T(8,128)(2,1)}, u32[]{:S(2)}) copy-start(bf16[128,256]{1,0:T(8,128)(2,1)} %param.12) | copy-start | bytes 196612
  (8 other events, 16.9 us)
Sparse Core Ops, SparseCore 0:
  9.6 52.1 all-gather.2
  63.9 125.1 all-gather.4
  223.8 148.4 reduce-scatter.4
  375.4 43.9 reduce-scatter.2
where the time goes:
time: 431 us; the launch traced here: 426 us
  waiting for transfers between devices  168 us (39%)
  local copies, waits for them, and re-layouts  87.2 us (20%)
  blocking collectives  54.5 us (13%)
  other arithmetic  49 us (11%)
  matrix products  32.8 us (8%)
  starting transfers between devices  20.3 us (5%)
  between operations  14.4 us (3%)
    all_gather x1, waiting for transfers between devices, local(): weight_block = lax.all_gather(value_weight, 'dp', axis=0, tiled=True)  98 us
    reduce_scatter x1, waiting for transfers between devices, local(): lax.psum_scatter(lax.dot_general(grad_values, weight_block, (((1,), (1,))...  42.6 us
    psum x1, blocking collectives, local(): lax.psum((short_grad * row_scale).astype(jnp.bfloat16), 'dp')  36.9 us
    unnamed x55, local copies, waits for them, and re-layouts  23.5 us
    reduce_sum x3, other arithmetic, conv_taps_grad(): jnp.sum(gradient * extended[conv_edge - shift_back:conv_edge - shift_back...  20.4 us
    all_to_all x1, waiting for transfers between devices, local(): lax.all_to_all(gate_out, 'ctx', split_axis=1, concat_axis=0, tiled=True)  19.7 us
    all_to_all x1, blocking collectives, local(): lax.all_to_all(out_block, 'ctx', split_axis=0, concat_axis=1, tiled=True)  17.6 us
    reshape x1, local copies, waits for them, and re-layouts, fold_table(): flat.reshape(group_count, filter_span, double_span + 1)  14.3 us
  transfers between devices with their start and end apart: 9, of which 4 were waited for; matrix products, arithmetic and copies ran while one was open for 33% of the time, Pallas kernels for 0%

commit v1 on v0

v1 whole, which is shorter than its diff:
```python
import functools
import math

import jax
import jax.numpy as jnp
from jax import lax
from jax.experimental import pallas as pl
from jax.experimental.pallas import tpu as pltpu
from jax.sharding import PartitionSpec as P

MESH = pl.DeviceIdType.MESH
ANY = pl.BlockSpec(memory_space=pl.ANY)
LANES = 128
CHUNK = 64


def greet(dp, ctx):
    me_dp, me_ctx = lax.axis_index("dp"), lax.axis_index("ctx")
    barrier = pltpu.get_barrier_semaphore()
    for step in range(1, dp):
        pl.semaphore_signal(
            barrier, inc=1, device_id=(lax.rem(me_dp + step, dp), me_ctx), device_id_type=MESH
        )
    for step in range(1, ctx):
        pl.semaphore_signal(
            barrier, inc=1, device_id=(me_dp, lax.rem(me_ctx + step, ctx)), device_id_type=MESH
        )
    pl.semaphore_wait(barrier, dp + ctx - 2)


def send(src, dst, send_sem, recv_sem, device):
    return pltpu.make_async_remote_copy(
        src_ref=src,
        dst_ref=dst,
        send_sem=send_sem,
        recv_sem=recv_sem,
        device_id=device,
        device_id_type=MESH,
    )


def gather_kernel(
    dp, ctx, pair,
    features, gate_in, gate_out, cot, weight,
    window, block_in, block_out, block_cot, full,
    local_sem, ctx_send, ctx_recv, right_send, left_send, pair_send, full_recv,
):
    me_dp, me_ctx = lax.axis_index("dp"), lax.axis_index("ctx")
    line = dp // pair
    at, side = me_dp // pair, lax.rem(me_dp, pair)
    rows = features.shape[0]
    cols, depth = weight.shape[1], weight.shape[0]
    greet(dp, ctx)

    def block(index):
        return full.at[pl.ds(pl.multiple_of(index * depth, depth), depth)]

    def push(src, index, sem, to):
        return send(src, block(index), sem, full_recv.at[index], (to, me_ctx))

    def others(index, src):
        if pair == 2:
            push(src, index, pair_send.at[index // pair], at * pair + 1 - side).start()

    @pl.when(at + 1 < line)
    def _():
        push(weight, me_dp, right_send.at[at], me_dp + pair).start()

    @pl.when(at > 0)
    def _():
        push(weight, me_dp, left_send.at[at], me_dp - pair).start()

    others(me_dp, weight)

    mine = pl.ds(pl.multiple_of(me_ctx * rows, rows), rows)
    streams = ((gate_in, block_in), (gate_out, block_out), (cot, block_cot))
    copies = []
    for which, (src, dst) in enumerate(((features, window),) + streams):
        for step in range(1, ctx):
            peer = lax.rem(me_ctx + step, ctx)
            part = src if which == 0 else src.at[:, pl.ds(pl.multiple_of(peer * cols, cols), cols)]
            copies.append(
                send(
                    part, dst.at[mine], ctx_send.at[which, step], ctx_recv.at[which, step],
                    (me_dp, peer),
                )
            )
            copies[-1].start()
    stays = [pltpu.make_async_copy(weight, block(me_dp), local_sem.at[4])]
    stays.append(pltpu.make_async_copy(features, window.at[mine], local_sem.at[0]))
    for which, (src, dst) in enumerate(streams):
        part = src.at[:, pl.ds(pl.multiple_of(me_ctx * cols, cols), cols)]
        stays.append(pltpu.make_async_copy(part, dst.at[mine], local_sem.at[which + 1]))
    for copy in stays:
        copy.start()

    def arrived(index):
        push(block(index), index, right_send.at[0], me_dp).wait_recv()

    for far in range(1, line):
        @pl.when(at - far >= 0)
        def _():
            index = me_dp - far * pair
            arrived(index)

            @pl.when(at + 1 < line)
            def _():
                push(block(index), index, right_send.at[at - far], me_dp + pair).start()

            others(index, block(index))

        @pl.when(at + far < line)
        def _():
            index = me_dp + far * pair
            arrived(index)

            @pl.when(at > 0)
            def _():
                push(block(index), index, left_send.at[at + far], me_dp - pair).start()

            others(index, block(index))

    for copy in copies:
        copy.wait()
    for copy in stays:
        copy.wait()
    for spot in range(line):
        if pair == 2:
            arrived(spot * pair + 1 - side)
            push(weight, me_dp, pair_send.at[spot], me_dp).wait_send()

        @pl.when((at + 1 < line) & (spot <= at))
        def _():
            push(weight, me_dp, right_send.at[spot], me_dp).wait_send()

        @pl.when((at > 0) & (spot >= at))
        def _():
            push(weight, me_dp, left_send.at[spot], me_dp).wait_send()


def gather_all(dp, ctx, features, gate_in, gate_out, cot, weight):
    pair = 2 if dp % 2 == 0 else 1
    rows, channels = features.shape
    depth, cols = weight.shape
    shapes = [(rows * ctx, channels)] + [(rows * ctx, cols)] * 3 + [(depth * dp, cols)]
    dma = pltpu.SemaphoreType.DMA
    line = dp // pair
    return pl.pallas_call(
        functools.partial(gather_kernel, dp, ctx, pair),
        out_shape=[jax.ShapeDtypeStruct(shape, jnp.bfloat16) for shape in shapes],
        in_specs=[ANY] * 5,
        out_specs=[ANY] * 5,
        scratch_shapes=[
            dma((5,)), dma((4, ctx)), dma((4, ctx)), dma((line,)), dma((line,)), dma((line,)),
            dma((dp,)),
        ],
        compiler_params=pltpu.CompilerParams(collective_id=0, has_side_effects=True),
    )(features, gate_in, gate_out, cot, weight)


def scatter_kernel(
    dp, ctx, pair,
    grad_weight, terms, layer, first, second, small,
    weight_out, terms_out, layer_out, first_out, second_out, small_out,
    held, from_pair, from_left, from_right,
    local_sem, held_sem, ctx_send, ctx_recv, small_send, small_recv,
    pair_send, pair_recv, right_send, left_recv, left_send, right_recv, out_sem,
):
    me_dp, me_ctx = lax.axis_index("dp"), lax.axis_index("ctx")
    line = dp // pair
    at, side = me_dp // pair, lax.rem(me_dp, pair)
    rows, cols = layer_out.shape[0], layer.shape[1]
    depth = weight_out.shape[0]
    greet(dp, ctx)

    def block(index):
        return grad_weight.at[pl.ds(pl.multiple_of(index * depth, depth), depth)]

    def keep(spot):
        return pltpu.make_async_copy(block(spot * pair + side), held.at[spot], held_sem.at[spot])

    def swap(spot):
        return send(
            block(spot * pair + 1 - side), from_pair.at[spot], pair_send.at[spot],
            pair_recv.at[spot], (at * pair + 1 - side, me_ctx),
        )

    def to_right(spot):
        return send(
            held.at[spot], from_left.at[spot], right_send.at[spot], left_recv.at[spot],
            (me_dp + pair, me_ctx),
        )

    def to_left(spot):
        return send(
            held.at[spot], from_right.at[spot], left_send.at[spot], right_recv.at[spot],
            (me_dp - pair, me_ctx),
        )

    def begin(spot):
        if pair == 2:
            swap(spot).start()
        keep(spot).start()

    for far in range(line - 1, 0, -1):
        pl.when(at + far < line)(functools.partial(begin, at + far))
        pl.when(at - far >= 0)(functools.partial(begin, at - far))
    begin(at)

    copies = []
    mine = pl.ds(pl.multiple_of(me_ctx * cols, cols), cols)
    for step in range(1, dp):
        peer = lax.rem(me_dp + step, dp)
        copies.append(
            send(small, small_out.at[me_dp], small_send.at[step], small_recv.at[step], (peer, me_ctx))
        )
    outs = ((layer, layer_out), (first, first_out), (second, second_out))
    for which, (src, dst) in enumerate(((terms, terms_out),) + outs):
        for step in range(1, ctx):
            peer = lax.rem(me_ctx + step, ctx)
            copies.append(
                send(
                    src.at[pl.ds(pl.multiple_of(peer * rows, rows), rows)],
                    dst.at[me_ctx] if which == 0 else dst.at[:, mine],
                    ctx_send.at[which, step], ctx_recv.at[which, step], (me_dp, peer),
                )
            )
        part = src.at[pl.ds(pl.multiple_of(me_ctx * rows, rows), rows)]
        copies.append(
            pltpu.make_async_copy(
                part, dst.at[me_ctx] if which == 0 else dst.at[:, mine], local_sem.at[which]
            )
        )
    copies.append(pltpu.make_async_copy(small, small_out.at[me_dp], local_sem.at[4]))
    for copy in copies:
        copy.start()

    span = 32

    def add(spot, source):
        def body(step, carry):
            part = pl.ds(pl.multiple_of(step * span, span), span)
            held[spot, part] = (
                held[spot, part].astype(jnp.float32) + source[spot, part].astype(jnp.float32)
            ).astype(jnp.bfloat16)
            return carry

        lax.fori_loop(0, depth // span, body, 0)

    def ready(spot):
        keep(spot).wait()
        if pair == 2:
            swap(spot).wait_recv()
            add(spot, from_pair)

    def go_right(spot):
        ready(spot)

        @pl.when(at > 0)
        def _():
            to_right(spot).wait_recv()
            add(spot, from_left)

        to_right(spot).start()

    def go_left(spot):
        ready(spot)

        @pl.when(at + 1 < line)
        def _():
            to_left(spot).wait_recv()
            add(spot, from_right)

        to_left(spot).start()

    for far in range(line - 1, 0, -1):
        pl.when(at + far < line)(functools.partial(go_right, at + far))
        pl.when(at - far >= 0)(functools.partial(go_left, at - far))
    ready(at)

    @pl.when(at > 0)
    def _():
        to_right(at).wait_recv()
        add(at, from_left)

    @pl.when(at + 1 < line)
    def _():
        to_left(at).wait_recv()
        add(at, from_right)

    result = pltpu.make_async_copy(held.at[at], weight_out, out_sem)
    result.start()
    for copy in copies:
        copy.wait()
    for spot in range(line):
        if pair == 2:
            swap(spot).wait_send()
        pl.when(spot > at)(lambda spot=spot: to_right(spot).wait_send())
        pl.when(spot < at)(lambda spot=spot: to_left(spot).wait_send())
    result.wait()


def scatter_all(dp, ctx, grad_weight, terms, layer, first, second, small):
    pair = 2 if dp % 2 == 0 else 1
    line = dp // pair
    length, cols = layer.shape
    rows, channels, depth = length // ctx, terms.shape[1], grad_weight.shape[0] // dp
    shapes = [(depth, cols), (ctx, rows, channels)] + [(rows, channels)] * 3 + [(dp,) + small.shape]
    dma = pltpu.SemaphoreType.DMA
    slots = pltpu.VMEM((line, depth, cols), jnp.bfloat16)
    return pl.pallas_call(
        functools.partial(scatter_kernel, dp, ctx, pair),
        out_shape=[jax.ShapeDtypeStruct(shape, jnp.bfloat16) for shape in shapes],
        in_specs=[ANY] * 6,
        out_specs=[ANY] * 6,
        scratch_shapes=[slots] * 4
        + [dma((5,)), dma((line,)), dma((4, ctx)), dma((4, ctx)), dma((dp,)), dma((dp,))]
        + [dma((line,))] * 6
        + [dma],
        compiler_params=pltpu.CompilerParams(
            collective_id=1, has_side_effects=True, vmem_limit_bytes=40 * 2**20
        ),
    )(grad_weight, terms, layer, first, second, small)


def mixer_kernel(
    group_width,
    gate_in, gate_out, values, cot, taps, ahead, behind,
    layer, grad_in, grad_out, grad_values, grad_short, grad_medium,
    streams, convs, grads, product, grad_filtered, table, back, filtered, grad_product,
):
    length = gate_in.shape[0]
    span = table.shape[1] // 2
    groups = LANES // group_width
    edge = taps.shape[1]
    f32, bf16 = jnp.float32, jnp.bfloat16
    streams[:, :8] = jnp.zeros((3, 8, LANES), f32)
    grads[:, length:] = jnp.zeros((3, 8, LANES), f32)
    product[:span] = jnp.zeros((span, LANES), bf16)
    grad_filtered[length:] = jnp.zeros((span, LANES), bf16)
    for index, stream in enumerate((gate_in, gate_out, values)):
        streams[index, 8:] = stream[...].astype(f32)

    for source, target in ((ahead, table), (behind, back)):
        for group in range(groups):
            rows = jnp.broadcast_to(source[group : group + 1], (8, 2 * span))
            offset = lax.broadcasted_iota(jnp.int32, (8, 2 * span), 0)
            for bit in (1, 2, 4):
                rows = jnp.where((offset & bit) != 0, pltpu.roll(rows, bit, 1), rows)
            height = 8
            while height < span:
                rows = jnp.concatenate([rows, pltpu.roll(rows, height, 1)], axis=0)
                height *= 2
            target[group * span : (group + 1) * span] = rows.astype(bf16)

    for base in range(0, length, CHUNK):
        part = slice(base, base + CHUNK)
        conv = []
        for index in range(3):
            running = taps[index, 0:1] * streams[index, 8 + base : 8 + base + CHUNK]
            for shift in range(1, edge):
                start = 8 + base - shift
                running = running + taps[index, shift : shift + 1] * streams[index, start : start + CHUNK]
            conv.append(running)
            convs[index, part] = running
        product[span + base : span + base + CHUNK] = (conv[0] * conv[2]).astype(bf16)
        grad_filtered[part] = (cot[part].astype(f32) * conv[1]).astype(bf16)

    owner = lax.broadcasted_iota(jnp.int32, (span, LANES), 1) // group_width
    for base in range(0, length, span):
        near = product[base : base + 2 * span]
        for matrix, window, target in (
            (table, near, filtered),
            (back, grad_filtered[base : base + 2 * span], grad_product),
        ):
            chosen = None
            for group in range(groups):
                out = jnp.dot(
                    matrix[group * span : (group + 1) * span], window, preferred_element_type=f32
                )
                chosen = out if chosen is None else jnp.where(owner == group, out, chosen)
            target[base : base + span] = chosen

    for group in range(groups):
        total = None
        for base in range(0, length, span):
            current = grad_filtered[base : base + span].astype(f32)
            current = jnp.where(owner == group, current, 0.0).astype(bf16)
            term = lax.dot_general(
                current, product[base : base + 2 * span], (((1,), (1,)), ((), ())),
                preferred_element_type=f32,
            )
            total = term if total is None else total + term
        height = span // 2
        while height >= 8:
            total = total[:height] + pltpu.roll(total[height:], 2 * span - height, 1)
            height //= 2
        offset = lax.broadcasted_iota(jnp.int32, (8, 2 * span), 0)
        for bit in (1, 2, 4):
            total = jnp.where((offset & bit) != 0, pltpu.roll(total, 2 * span - bit, 1), total)
        grad_medium[group : group + 1] = jnp.sum(total, axis=0, keepdims=True)

    for base in range(0, length, CHUNK):
        part = slice(base, base + CHUNK)
        kept = filtered[part]
        gradient = grad_product[part]
        layer[part] = (convs[1, part] * kept).astype(bf16)
        grads[0, part] = gradient * convs[2, part]
        grads[1, part] = cot[part].astype(f32) * kept
        grads[2, part] = gradient * convs[0, part]

    outs = (grad_in, grad_out, grad_values)
    for index in range(3):
        tap_sums = [jnp.zeros((8, LANES), f32) for _ in range(edge)]
        for base in range(0, length, CHUNK):
            stream = streams[index, 8 + base : 8 + base + CHUNK]
            running = None
            for shift in range(edge):
                gradient = grads[index, base + shift : base + shift + CHUNK]
                term = taps[index, shift : shift + 1] * gradient
                running = term if running is None else running + term
                tap_sums[shift] = tap_sums[shift] + jnp.sum(
                    (gradient * stream).reshape(CHUNK // 8, 8, LANES), axis=0
                )
            outs[index][base : base + CHUNK] = running.astype(bf16)
        for shift in range(edge):
            grad_short[index, shift : shift + 1] = jnp.sum(tap_sums[shift], axis=0, keepdims=True)


def mixer(gate_in, gate_out, values, cot, taps, medium, group_width):
    length, cols = gate_in.shape
    span, group_count = medium.shape
    edge = taps.shape[1]
    lifted = medium.astype(jnp.float32).T
    zeros = jnp.zeros((group_count, span), jnp.float32)
    ahead = jnp.concatenate([zeros[:, :1], lifted[:, ::-1], zeros[:, 1:]], axis=1)
    behind = jnp.concatenate([lifted, zeros], axis=1)
    groups = LANES // group_width
    rows = pl.BlockSpec((length, LANES), lambda i: (0, i))
    taps_spec = pl.BlockSpec((3, edge, LANES), lambda i: (0, 0, i))
    group_spec = pl.BlockSpec((groups, 2 * span), lambda i: (i, 0))
    f32, bf16 = jnp.float32, jnp.bfloat16
    outs = pl.pallas_call(
        functools.partial(mixer_kernel, group_width),
        grid=(cols // LANES,),
        out_shape=[jax.ShapeDtypeStruct((length, cols), bf16)] * 4
        + [
            jax.ShapeDtypeStruct((3, edge, cols), f32),
            jax.ShapeDtypeStruct((group_count, 2 * span), f32),
        ],
        in_specs=[rows] * 4 + [taps_spec, group_spec, group_spec],
        out_specs=[rows] * 4 + [taps_spec, group_spec],
        scratch_shapes=[
            pltpu.VMEM((3, length + 8, LANES), f32),
            pltpu.VMEM((3, length, LANES), f32),
            pltpu.VMEM((3, length + 8, LANES), f32),
            pltpu.VMEM((length + span, LANES), bf16),
            pltpu.VMEM((length + span, LANES), bf16),
            pltpu.VMEM((groups * span, 2 * span), bf16),
            pltpu.VMEM((groups * span, 2 * span), bf16),
            pltpu.VMEM((length, LANES), f32),
            pltpu.VMEM((length, LANES), f32),
        ],
        compiler_params=pltpu.CompilerParams(vmem_limit_bytes=40 * 2**20),
    )(gate_in, gate_out, values, cot, taps, ahead, behind)
    return (*outs[:5], outs[5][:, 1 : span + 1][:, ::-1].T)


def local(features, gate_in, gate_out, value_weight, short_taps, medium_taps, cotangent):
    ctx = lax.axis_size("ctx")
    dp = lax.axis_size("dp")
    ctx_index = lax.axis_index("ctx")
    rows, channels = features.shape
    cols = value_weight.shape[1]
    span, group_count = medium_taps.shape
    group_width = channels // group_count
    total_rows = rows * ctx * dp
    row_scale = 1.0 / math.sqrt(total_rows)
    group_scale = 1.0 / math.sqrt(total_rows * group_width)
    f32, bf16 = jnp.float32, jnp.bfloat16
    taps = lax.dynamic_slice_in_dim(short_taps, ctx_index * cols, cols, 2)
    own_groups = group_count // ctx
    medium = lax.dynamic_slice_in_dim(medium_taps, ctx_index * own_groups, own_groups, 1)
    window, block_in, block_out, block_cot, weight = gather_all(
        dp, ctx, features, gate_in, gate_out, cotangent, value_weight
    )
    values = jnp.dot(window, weight, preferred_element_type=f32).astype(bf16)
    layer, grad_in, grad_out, grad_values, grad_short, grad_medium = mixer(
        block_in, block_out, values, block_cot, taps, medium, group_width
    )
    grad_weight = (
        lax.dot_general(window, grad_values, (((0,), (0,)), ((), ())), preferred_element_type=f32)
        * row_scale
    ).astype(bf16)
    terms = lax.dot_general(
        grad_values, weight, (((1,), (1,)), ((), ())), preferred_element_type=f32
    ).astype(bf16)
    short_size, medium_size = grad_short.size, grad_medium.size
    flat = jnp.concatenate(
        [(grad_short * row_scale).reshape(-1), (grad_medium * group_scale).reshape(-1)]
    )
    pad = -flat.size % (16 * cols)
    small = jnp.pad(flat, (0, pad)).astype(bf16).reshape(-1, cols)
    weight_out, terms_out, layer_out, first_out, second_out, small_out = scatter_all(
        dp, ctx, grad_weight, terms, layer, grad_in, grad_out, small
    )
    grad_features = jnp.sum(terms_out.astype(f32), axis=0).astype(bf16)
    sums = jnp.sum(small_out.astype(f32), axis=0).reshape(-1)
    return (
        layer_out,
        grad_features,
        first_out,
        second_out,
        weight_out,
        sums[:short_size].reshape(grad_short.shape),
        sums[short_size : short_size + medium_size].reshape(grad_medium.shape),
    )


def solution(mesh):
    rows, split = P(("dp", "ctx"), None), P("dp", "ctx")
    return jax.shard_map(
        local,
        mesh=mesh,
        in_specs=(rows, rows, rows, split, P(), P(), rows),
        out_specs=(rows, rows, rows, rows, split, P(None, None, "ctx"), P(None, "ctx")),
        check_vma=False,
    )
```

time: 431 us -> 285 us (0.66); the launches traced: 426 us -> 285 us
  Pallas kernels: 0 us -> 236 us
  waiting for transfers between devices: 168 us -> 0 us
  local copies, waits for them, and re-layouts: 87.2 us -> 19.1 us
  blocking collectives: 54.5 us -> 0 us
  other arithmetic: 49 us -> 4.43 us
  starting transfers between devices: 20.3 us -> 0 us
  between operations: 14.4 us -> 0.87 us
  matrix products: 32.8 us -> 24.6 us
    pallas_call x0 -> x3, Pallas kernels: none -> 236 us  [the longest x1 102 us: gather_all(): pl.pallas_call(functools.partial(gather_kernel, dp, ctx, pair), out_shape...]
    all_gather x2 -> x0, waiting for transfers between devices: 98 us -> none  [the longest x1 98 us: local(): weight_block = lax.all_gather(value_weight, 'dp', axis=0, tiled=True)]
    reduce_scatter x2 -> x0, waiting for transfers between devices: 42.6 us -> none  [the longest x1 42.6 us: local(): lax.psum_scatter(lax.dot_general(grad_values, weight_block, (((1,), (1,))...]
    psum x1 -> x0, blocking collectives: 36.9 us -> none  [local(): lax.psum((short_grad * row_scale).astype(jnp.bfloat16), 'dp')]
    all_to_all x5 -> x0, waiting for transfers between devices: 25.8 us -> none  [the longest x1 19.7 us: local(): lax.all_to_all(gate_out, 'ctx', split_axis=1, concat_axis=0, tiled=True)]
    reduce_sum x4 -> x2, other arithmetic: 26.7 us -> 4.3 us  [the longest x1 4.22 us: local(): grad_features = jnp.sum(terms_out.astype(f32), axis=0).astype(bf16)]
    convert_element_type x9 -> x0, other arithmetic: 22.2 us -> none  [the longest x2 8.95 us: mixer_pass(): grad_filtered = (cot_rows * convs[1]).astype(jnp.bfloat16)]
    reshape x7 -> x5, local copies, waits for them, and re-layouts: 24.3 us -> 3.84 us  [the longest x1 1.54 us: local(): sums[:short_size].reshape(grad_short.shape)]
  transfers between devices with their start and end apart: 9 -> 0, of which waited for: 4 -> 0; matrix products, arithmetic and copies ran while one was open for 33% -> 0% of each run, Pallas kernels for 0% -> 0%
where the time goes in v1:
time: 285 us
  Pallas kernels  236 us (83%)
  matrix products  24.6 us (9%)
  local copies, waits for them, and re-layouts  19.1 us (7%)
  other arithmetic  4.43 us (2%)
    pallas_call x1, Pallas kernels, gather_all(): pl.pallas_call(functools.partial(gather_kernel, dp, ctx, pair), out_shape...  102 us
    pallas_call x1, Pallas kernels, scatter_all(): pl.pallas_call(functools.partial(scatter_kernel, dp, ctx, pair), out_shap...  101 us
    pallas_call x1, Pallas kernels, mixer(): pl.pallas_call(functools.partial(mixer_kernel, group_width), grid=(cols /...  33.4 us
    unnamed x34, local copies, waits for them, and re-layouts  12.7 us
    dot_general x1, matrix products, local(): values = jnp.dot(window, weight, preferred_element_type=f32).astype(bf16)  9.28 us
    dot_general x1, matrix products, local(): lax.dot_general(window, grad_values, (((0,), (0,)), ((), ())), preferred_...  9.21 us
    dot_general x1, matrix products, local(): lax.dot_general(grad_values, weight, (((1,), (1,)), ((), ())), preferred_...  6.09 us

profile of v1, /device:TPU:0, one launch (start us, length us, event | category | flops | bytes accessed | tf_op | source)
XLA Modules:
  0.0 284.6 jit_solution(16022976807695426729)
XLA Ops:
  0.7 0.9 constant_dynamic-slice_fusion
  1.9 101.6 %shard_map.126 = (bf16[512,4096]{1,0:T(8,128)(2,1)}, bf16[512,1024]{1,0:T(8,128)(2,1)}, bf16[512,1024]{1,0:T(8,128)(2,1)}, bf16[512,1024]{1,0:T(8,128)(2,1)}, bf16[4096,1024]{1,0:T(8,128)(2,1)}) custom-call(bf16[128,4096]{1,0:T(8,128)(2,1)} %features.1, bf16[128,4096]{1,0:T(8,128)(2,1)} %gate_in.1, bf16[128,4096]{1,0:T(8,128)(2,1)} %gate_out.1, ...), custom_call_target="tpu_custom_call" | custom-call | tf_op jit(solution)/shard_map/pallas_call | solution.py:148
  103.6 9.3 %convolution_convert_fusion.1.values = bf16[512,1024]{1,0:T(8,128)(2,1)S(1)} fusion(bf16[512,4096]{1,0:T(8,128)(2,1)} %get-tuple-element.24, bf16[4096,1024]{1,0:T(8,128)(2,1)} %get-tuple-element.27), kind=kOutput, calls=%fused_computation.2 | convolution fusion | flops 4295491584 | bytes 13631488 | tf_op jit(solution)/shard_map/dot_general | solution.py:487
  112.9 33.4 %shard_map.127 = (bf16[512,1024]{1,0:T(8,128)(2,1)S(1)}, bf16[512,1024]{1,0:T(8,128)(2,1)S(1)}, bf16[512,1024]{1,0:T(8,128)(2,1)S(1)}, bf16[512,1024]{1,0:T(8,12...) custom-call(bf16[512,1024]{1,0:T(8,128)(2,1)S(1)} %copy-done.3, bf16[512,1024]{1,0:T(8,128)(2,1)S(1)} %copy-done.4, ...), custom_call_target="tpu_custom_call" | custom-call | tf_op jit(solution)/shard_map/pallas_call | solution.py:443
  146.4 1.0 copy-done.6
  147.3 1.0 copy-done.8
  148.3 1.0 copy-done.10
  149.3 6.1 %convolution_convert_fusion.terms = bf16[512,4096]{1,0:T(8,128)(2,1)} fusion(bf16[512,1024]{1,0:T(8,128)(2,1)S(1)} %get-tuple-element.29, bf16[4096,1024]{1,0:T(8,128)(2,1)S(1)} %copy-done.13), kind=kOutput, calls=%fused_computation.1 | convolution fusion | flops 4297064448 | bytes 13631488 | tf_op jit(solution)/shard_map/dot_general | solution.py:495
  155.5 0.1 copy.16
  155.9 0.7 reshape.38.small
  156.5 9.2 %multiply_convert_fusion.grad_weight = bf16[4096,1024]{1,0:T(8,128)(2,1)} fusion(bf16[512,4096]{1,0:T(8,128)(2,1)} %get-tuple-element.24, bf16[512,1024]{1,0:T(8,128)(2,1)S(1)} %get-tuple-element.29), kind=kOutput, calls=%fused_computation | convolution fusion | flops 4303355904 | bytes 13631488 | tf_op jit(solution)/shard_map/dot_general | solution.py:492
  165.8 100.6 %shard_map.128 = (bf16[512,1024]{1,0:T(8,128)(2,1)S(1)}, bf16[4,128,4096]{2,1,0:T(8,128)(2,1)S(1)}, bf16[128,4096]{1,0:T(8,128)(2,1)S(1)}, bf16[128,4096]{1,0:T(...) custom-call(bf16[4096,1024]{1,0:T(8,128)(2,1)} %multiply_convert_fusion.grad_weight, ...), custom_call_target="tpu_custom_call" | custom-call | tf_op jit(solution)/shard_map/pallas_call | solution.py:311
  266.4 1.9 copy-done.1
  268.3 1.0 copy-done.2
  269.4 0.6 slice.23
  270.0 0.6 slice.22
  270.7 1.5 reshape.39
  272.2 1.5 reshape.40
  273.7 1.5 copy.17
  275.2 4.2 %reduce_sum.21 = bf16[128,4096]{1,0:T(8,128)(2,1)} reduce(bf16[4,128,4096]{2,1,0:T(8,128)(2,1)} %copy-done.1, bf16[]{:T(256)} %constant.9.clone.1), dimensions={0}, to_apply=%region_0.1 | reduce | flops 1572864 | bytes 5242882 | tf_op jit(solution)/shard_map/reduce_sum | solution.py:507
  279.4 2.3 copy.23
  281.7 1.0 copy.24
  282.7 1.0 copy.25
  283.7 1.0 copy.26
  (40 shorter events, 0.8 us)
Async XLA Ops:
  0.6 1.3 copy-start
  103.6 9.3 %copy-start.3 = (bf16[512,1024]{1,0:T(8,128)(2,1)S(1)}, bf16[512,1024]{1,0:T(8,128)(2,1)}, u32[]{:S(2)}) copy-start(bf16[512,1024]{1,0:T(8,128)(2,1)} %get-tuple-element.25.gate_in) | copy-start | bytes 3145732
  103.6 9.3 %copy-start.4 = (bf16[512,1024]{1,0:T(8,128)(2,1)S(1)}, bf16[512,1024]{1,0:T(8,128)(2,1)}, u32[]{:S(2)}) copy-start(bf16[512,1024]{1,0:T(8,128)(2,1)} %get-tuple-element.26.gate_out) | copy-start | bytes 3145732
  103.6 9.3 %copy-start.5 = (bf16[512,1024]{1,0:T(8,128)(2,1)S(1)}, bf16[512,1024]{1,0:T(8,128)(2,1)}, u32[]{:S(2)}) copy-start(bf16[512,1024]{1,0:T(8,128)(2,1)} %get-tuple-element.28.cot) | copy-start | bytes 3145732
  103.6 45.6 %copy-start.13 = (bf16[4096,1024]{1,0:T(8,128)(2,1)S(1)}, bf16[4096,1024]{1,0:T(8,128)(2,1)}, u32[]{:S(2)}) copy-start(bf16[4096,1024]{1,0:T(8,128)(2,1)} %get-tuple-element.27) | copy-start | bytes 25165828
  146.3 1.0 copy-start.6
  147.3 1.0 copy-start.8
  148.3 1.0 copy-start.10
  156.5 9.2 %copy-start.7 = (bf16[512,1024]{1,0:T(8,128)(2,1)S(1)}, bf16[512,1024]{1,0:T(8,128)(2,1)}, u32[]{:S(2)}) copy-start(bf16[512,1024]{1,0:T(8,128)(2,1)} %copy-done.6) | copy-start | bytes 3145732
  156.5 9.2 %copy-start.9 = (bf16[512,1024]{1,0:T(8,128)(2,1)S(1)}, bf16[512,1024]{1,0:T(8,128)(2,1)}, u32[]{:S(2)}) copy-start(bf16[512,1024]{1,0:T(8,128)(2,1)} %copy-done.8) | copy-start | bytes 3145732
  156.5 9.2 %copy-start.11 = (bf16[512,1024]{1,0:T(8,128)(2,1)S(1)}, bf16[512,1024]{1,0:T(8,128)(2,1)}, u32[]{:S(2)}) copy-start(bf16[512,1024]{1,0:T(8,128)(2,1)} %copy-done.10) | copy-start | bytes 3145732
  156.5 9.2 %copy-start.12 = (bf16[32,1024]{1,0:T(8,128)(2,1)S(1)}, bf16[32,1024]{1,0:T(8,128)(2,1)}, u32[]{:S(2)}) copy-start(bf16[32,1024]{1,0:T(8,128)(2,1)} %reshape.38.small) | copy-start | bytes 196612
  266.4 2.0 copy-start.1
  268.3 1.0 copy-start.2

commit v2 on v1

v2 whole, which is shorter than its diff:
```python
import functools
import math

import jax
import jax.numpy as jnp
from jax import lax
from jax.experimental import pallas as pl
from jax.experimental.pallas import tpu as pltpu
from jax.sharding import PartitionSpec as P

MESH = pl.DeviceIdType.MESH
ANY = pl.BlockSpec(memory_space=pl.ANY)
LANES = 128
CHUNK = 64
VMEM = pl.BlockSpec(memory_space=pltpu.VMEM)
F32, BF16 = jnp.float32, jnp.bfloat16


def greet(dp, ctx):
    me_dp, me_ctx = lax.axis_index("dp"), lax.axis_index("ctx")
    barrier = pltpu.get_barrier_semaphore()
    for step in range(1, dp):
        pl.semaphore_signal(
            barrier, inc=1, device_id=(lax.rem(me_dp + step, dp), me_ctx), device_id_type=MESH
        )
    for step in range(1, ctx):
        pl.semaphore_signal(
            barrier, inc=1, device_id=(me_dp, lax.rem(me_ctx + step, ctx)), device_id_type=MESH
        )
    pl.semaphore_wait(barrier, dp + ctx - 2)


def send(src, dst, send_sem, recv_sem, device):
    return pltpu.make_async_remote_copy(
        src_ref=src,
        dst_ref=dst,
        send_sem=send_sem,
        recv_sem=recv_sem,
        device_id=device,
        device_id_type=MESH,
    )


def spread(source, target, groups, span):
    offset = lax.broadcasted_iota(jnp.int32, (8, 2 * span), 0)
    for group in range(groups):
        rows = jnp.broadcast_to(source[group : group + 1], (8, 2 * span))
        for bit in (1, 2, 4):
            rows = jnp.where((offset & bit) != 0, pltpu.roll(rows, bit, 1), rows)
        height = 8
        while height < span:
            rows = jnp.concatenate([rows, pltpu.roll(rows, height, 1)], axis=0)
            height *= 2
        target[group * span : (group + 1) * span] = rows.astype(BF16)


def filter_back(table, source, target, length, groups, span, owner):
    for base in range(0, length, span):
        chosen = None
        for group in range(groups):
            out = jnp.dot(
                table[group * span : (group + 1) * span], source[base : base + 2 * span],
                preferred_element_type=F32,
            )
            chosen = out if chosen is None else jnp.where(owner == group, out, chosen)
        target[base : base + span] = chosen


def ahead_conv(taps, index, stream, base, edge):
    running = taps[index, 0:1] * stream[8 + base : 8 + base + CHUNK]
    for shift in range(1, edge):
        start = 8 + base - shift
        running = running + taps[index, shift : shift + 1] * stream[start : start + CHUNK]
    return running


def clear(scratch, length, span):
    streams, _, grads, product, grad_filtered = scratch[:5]
    streams[:, :8] = jnp.zeros((3, 8, LANES), F32)
    grads[:, length:] = jnp.zeros((3, 8, LANES), F32)
    product[:span] = jnp.zeros((span, LANES), BF16)
    grad_filtered[length:] = jnp.zeros((span, LANES), BF16)


def values_gradient(group_width, gate_in, gate_out, cot, taps, behind, grad_values, scratch):
    streams, convs, grads, _, grad_filtered, _, back, _, grad_product = scratch
    length, edge, span = gate_in.shape[0], taps.shape[1], back.shape[1] // 2
    groups = LANES // group_width
    streams[0, 8:] = gate_in[...].astype(F32)
    streams[1, 8:] = gate_out[...].astype(F32)
    spread(behind, back, groups, span)
    for base in range(0, length, CHUNK):
        part = slice(base, base + CHUNK)
        convs[0, part] = ahead_conv(taps, 0, streams.at[0], base, edge)
        conv = ahead_conv(taps, 1, streams.at[1], base, edge)
        grad_filtered[part] = (cot[part].astype(F32) * conv).astype(BF16)
    owner = lax.broadcasted_iota(jnp.int32, (span, LANES), 1) // group_width
    filter_back(back, grad_filtered, grad_product, length, groups, span, owner)
    grads[2, :length] = grad_product[...] * convs[0]
    for base in range(0, length, CHUNK):
        running = taps[2, 0:1] * grads[2, base : base + CHUNK]
        for shift in range(1, edge):
            start = base + shift
            running = running + taps[2, shift : shift + 1] * grads[2, start : start + CHUNK]
        grad_values[base : base + CHUNK] = running.astype(BF16)


def mixer_block(
    group_width, gate_in, gate_out, values, cot, taps, ahead, behind,
    layer, grad_in, grad_out, grad_short, grad_medium, scratch,
):
    streams, convs, grads, product, grad_filtered, table, back, filtered, grad_product = scratch
    length, edge, span = gate_in.shape[0], taps.shape[1], back.shape[1] // 2
    groups = LANES // group_width
    for index, stream in enumerate((gate_in, gate_out, values)):
        streams[index, 8:] = stream[...].astype(F32)
    spread(ahead, table, groups, span)
    spread(behind, back, groups, span)
    for base in range(0, length, CHUNK):
        part = slice(base, base + CHUNK)
        conv = [ahead_conv(taps, index, streams.at[index], base, edge) for index in range(3)]
        for index in range(3):
            convs[index, part] = conv[index]
        product[span + base : span + base + CHUNK] = (conv[0] * conv[2]).astype(BF16)
        grad_filtered[part] = (cot[part].astype(F32) * conv[1]).astype(BF16)
    owner = lax.broadcasted_iota(jnp.int32, (span, LANES), 1) // group_width
    filter_back(table, product, filtered, length, groups, span, owner)
    filter_back(back, grad_filtered, grad_product, length, groups, span, owner)
    offset = lax.broadcasted_iota(jnp.int32, (8, 2 * span), 0)
    for group in range(groups):
        total = None
        for base in range(0, length, span):
            current = grad_filtered[base : base + span].astype(F32)
            current = jnp.where(owner == group, current, 0.0).astype(BF16)
            term = lax.dot_general(
                current, product[base : base + 2 * span], (((1,), (1,)), ((), ())),
                preferred_element_type=F32,
            )
            total = term if total is None else total + term
        height = span // 2
        while height >= 8:
            total = total[:height] + pltpu.roll(total[height:], 2 * span - height, 1)
            height //= 2
        for bit in (1, 2, 4):
            total = jnp.where((offset & bit) != 0, pltpu.roll(total, 2 * span - bit, 1), total)
        total = pltpu.roll(total, 2 * span - 1, 1)
        grad_medium[group : group + 1] = jnp.sum(total, axis=0, keepdims=True)[:, :span]
    for base in range(0, length, CHUNK):
        part = slice(base, base + CHUNK)
        kept = filtered[part]
        gradient = grad_product[part]
        layer[part] = (convs[1, part] * kept).astype(BF16)
        grads[0, part] = gradient * convs[2, part]
        grads[1, part] = cot[part].astype(F32) * kept
        grads[2, part] = gradient * convs[0, part]
    outs = (grad_in, grad_out, None)
    for index in range(3):
        tap_sums = [jnp.zeros((8, LANES), F32) for _ in range(edge)]
        for base in range(0, length, CHUNK):
            stream = streams[index, 8 + base : 8 + base + CHUNK]
            running = None
            for shift in range(edge):
                gradient = grads[index, base + shift : base + shift + CHUNK]
                if index < 2:
                    term = taps[index, shift : shift + 1] * gradient
                    running = term if running is None else running + term
                tap_sums[shift] = tap_sums[shift] + jnp.sum(
                    (gradient * stream).reshape(CHUNK // 8, 8, LANES), axis=0
                )
            if index < 2:
                outs[index][base : base + CHUNK] = running.astype(BF16)
        for shift in range(edge):
            grad_short[8 * index + shift : 8 * index + shift + 1] = jnp.sum(
                tap_sums[shift], axis=0, keepdims=True
            )


def mixer_scratch(length, span, group_width):
    groups = LANES // group_width
    f32, bf16 = (lambda *shape: pltpu.VMEM(shape, F32)), (lambda *shape: pltpu.VMEM(shape, BF16))
    return [
        f32(3, length + 8, LANES), f32(3, length, LANES), f32(3, length + 8, LANES),
        bf16(length + span, LANES), bf16(length + span, LANES),
        bf16(groups * span, 2 * span), bf16(groups * span, 2 * span),
        f32(length, LANES), f32(length, LANES),
    ]


def lane_block(step):
    return pl.ds(pl.multiple_of(step * LANES, LANES), LANES)


def group_rows(step, groups):
    return pl.ds(pl.multiple_of(step * groups, groups), groups)


def gather_kernel(
    dp, ctx, pair,
    group_width,
    features, gate_in, gate_out, cot, weight, taps, behind,
    window_out, in_out, out_out, cot_out, values, grad_values, terms,
    window, block_in, block_out, block_cot, full, total,
    local_sem, ctx_send, ctx_recv, right_send, left_send, pair_send, full_recv, out_sem,
    *scratch,
):
    me_dp, me_ctx = lax.axis_index("dp"), lax.axis_index("ctx")
    line = dp // pair
    at, side = me_dp // pair, lax.rem(me_dp, pair)
    rows = features.shape[0]
    cols, depth = weight.shape[1], weight.shape[0]
    greet(dp, ctx)

    def block(index):
        return full.at[index]

    def push(src, index, sem, to):
        return send(src, block(index), sem, full_recv.at[index], (to, me_ctx))

    def others(index, src):
        if pair == 2:
            push(src, index, pair_send.at[index // pair], at * pair + 1 - side).start()

    @pl.when(at + 1 < line)
    def _():
        push(weight, me_dp, right_send.at[at], me_dp + pair).start()

    @pl.when(at > 0)
    def _():
        push(weight, me_dp, left_send.at[at], me_dp - pair).start()

    others(me_dp, weight)

    mine = pl.ds(pl.multiple_of(me_ctx * rows, rows), rows)
    streams = ((gate_in, block_in), (gate_out, block_out), (cot, block_cot))
    copies = {}
    for which, (src, dst) in enumerate(((features, window),) + streams):
        copies[which] = []
        for step in range(1, ctx):
            peer = lax.rem(me_ctx + step, ctx)
            part = src if which == 0 else src.at[:, pl.ds(pl.multiple_of(peer * cols, cols), cols)]
            copies[which].append(
                send(
                    part, dst.at[mine], ctx_send.at[which, step], ctx_recv.at[which, step],
                    (me_dp, peer),
                )
            )
    for which in (1, 2, 3):
        for copy in copies[which]:
            copy.start()
    stays = [pltpu.make_async_copy(weight, block(me_dp), local_sem.at[4])]
    stays.append(pltpu.make_async_copy(features, window.at[mine], local_sem.at[0]))
    for which, (src, dst) in enumerate(streams):
        part = src.at[:, pl.ds(pl.multiple_of(me_ctx * cols, cols), cols)]
        stays.append(pltpu.make_async_copy(part, dst.at[mine], local_sem.at[which + 1]))
    for copy in stays:
        copy.start()

    def arrived(index):
        push(block(index), index, right_send.at[0], me_dp).wait_recv()

    def relay(far):
        @pl.when(at - far >= 0)
        def _():
            index = me_dp - far * pair
            arrived(index)

            @pl.when(at + 1 < line)
            def _():
                push(block(index), index, right_send.at[at - far], me_dp + pair).start()

            others(index, block(index))

        @pl.when(at + far < line)
        def _():
            index = me_dp + far * pair
            arrived(index)

            @pl.when(at > 0)
            def _():
                push(block(index), index, left_send.at[at + far], me_dp - pair).start()

            others(index, block(index))

    steps = cols // LANES
    groups = LANES // group_width
    length = window.shape[0]
    clear(scratch, length, scratch[6].shape[1] // 2)

    def gradient_step(step, carry):
        lanes = lane_block(step)
        values_gradient(
            group_width, block_in.at[:, lanes], block_out.at[:, lanes], block_cot.at[:, lanes],
            taps.at[:, :, lanes], behind.at[group_rows(step, groups)], grad_values.at[:, lanes],
            scratch,
        )
        return carry

    def add_terms(index):
        part = pl.ds(pl.multiple_of(index * depth, depth), depth)
        terms[:, part] = lax.dot_general(
            grad_values[...], full[index], (((1,), (1,)), ((), ())), preferred_element_type=F32
        ).astype(BF16)

    def add_values(index):
        part = pl.ds(pl.multiple_of(index * depth, depth), depth)
        total[...] += jnp.dot(window[:, part], full[index], preferred_element_type=F32)

    if line > 1:
        relay(1)
    for which in (1, 2, 3):
        for copy in copies[which]:
            copy.wait()
    for copy in copies[0]:
        copy.start()
    for copy in stays:
        copy.wait()
    leaves = [
        pltpu.make_async_copy(src, dst, out_sem.at[which])
        for which, (src, dst) in enumerate(
            ((block_in, in_out), (block_out, out_out), (block_cot, cot_out), (window, window_out))
        )
    ]
    for leave in leaves[:3]:
        leave.start()
    total[...] = jnp.zeros_like(total)
    lax.fori_loop(0, steps // 2, gradient_step, 0)
    if line > 2:
        relay(2)
    lax.fori_loop(steps // 2, steps, gradient_step, 0)
    for far in range(3, line):
        relay(far)

    def near_terms(spot, carry):
        add_terms(spot * pair + side)
        return carry

    def near_values(spot, carry):
        add_values(spot * pair + side)
        return carry

    def far_both(step, carry):
        index = lax.rem(at + step, line) * pair + 1 - side
        arrived(index)
        add_terms(index)
        add_values(index)
        return carry

    lax.fori_loop(0, line, near_terms, 0)
    for copy in copies[0]:
        copy.wait()
    leaves[3].start()
    lax.fori_loop(0, line, near_values, 0)
    if pair == 2:
        lax.fori_loop(0, line, far_both, 0)
    values[...] = total[...].astype(BF16)
    for leave in leaves:
        leave.wait()
    for spot in range(line):
        if pair == 2:
            push(weight, me_dp, pair_send.at[spot], me_dp).wait_send()

        @pl.when((at + 1 < line) & (spot <= at))
        def _():
            push(weight, me_dp, right_send.at[spot], me_dp).wait_send()

        @pl.when((at > 0) & (spot >= at))
        def _():
            push(weight, me_dp, left_send.at[spot], me_dp).wait_send()


def gather_all(dp, ctx, group_width, features, gate_in, gate_out, cot, weight, taps, behind):
    pair = 2 if dp % 2 == 0 else 1
    rows, channels = features.shape
    depth, cols = weight.shape
    length = rows * ctx
    span = behind.shape[1] // 2
    shapes = [(length, channels)] + [(length, cols)] * 5 + [(length, channels)]
    dma = pltpu.SemaphoreType.DMA
    line = dp // pair
    block = pltpu.VMEM((length, cols), BF16)
    return pl.pallas_call(
        functools.partial(gather_kernel, dp, ctx, pair, group_width),
        out_shape=[jax.ShapeDtypeStruct(shape, BF16) for shape in shapes],
        in_specs=[ANY] * 5 + [VMEM] * 2,
        out_specs=[ANY] * 4 + [VMEM] * 3,
        scratch_shapes=[
            pltpu.VMEM((length, channels), BF16), block, block, block,
            pltpu.VMEM((dp, depth, cols), BF16), pltpu.VMEM((length, cols), F32),
            dma((5,)), dma((4, ctx)), dma((4, ctx)), dma((line,)), dma((line,)), dma((line,)),
            dma((dp,)), dma((4,)),
        ]
        + mixer_scratch(length, span, group_width),
        compiler_params=pltpu.CompilerParams(
            collective_id=0, has_side_effects=True, vmem_limit_bytes=50 * 2**20
        ),
    )(features, gate_in, gate_out, cot, weight, taps, behind)


def scatter_kernel(
    dp, ctx, pair,
    group_width, row_scale, group_scale,
    grad_weight, terms, gate_in, gate_out, values, cot, taps, ahead, behind,
    weight_out, features_out, layer_out, first_out, second_out, short_out, medium_out,
    held, from_pair, from_left, from_right,
    terms_in, layer, first, second, short, medium, short_send, medium_send, short_in, medium_in,
    local_sem, held_sem, ctx_send, ctx_recv, small_send, small_recv,
    pair_send, pair_recv, right_send, left_recv, left_send, right_recv, out_sem,
    *scratch,
):
    me_dp, me_ctx = lax.axis_index("dp"), lax.axis_index("ctx")
    line = dp // pair
    at, side = me_dp // pair, lax.rem(me_dp, pair)
    rows, cols = layer_out.shape[0], layer.shape[1]
    depth = weight_out.shape[0]
    greet(dp, ctx)

    def block(index):
        return grad_weight.at[pl.ds(pl.multiple_of(index * depth, depth), depth)]

    def keep(spot):
        return pltpu.make_async_copy(block(spot * pair + side), held.at[spot], held_sem.at[spot])

    def swap(spot):
        return send(
            block(spot * pair + 1 - side), from_pair.at[spot], pair_send.at[spot],
            pair_recv.at[spot], (at * pair + 1 - side, me_ctx),
        )

    def to_right(spot):
        return send(
            held.at[spot], from_left.at[spot], right_send.at[spot], left_recv.at[spot],
            (me_dp + pair, me_ctx),
        )

    def to_left(spot):
        return send(
            held.at[spot], from_right.at[spot], left_send.at[spot], right_recv.at[spot],
            (me_dp - pair, me_ctx),
        )

    def begin(spot):
        if pair == 2:
            swap(spot).start()
        keep(spot).start()

    for far in range(line - 1, 0, -1):
        pl.when(at + far < line)(functools.partial(begin, at + far))
        pl.when(at - far >= 0)(functools.partial(begin, at - far))
    begin(at)

    copies = {}
    mine = pl.ds(pl.multiple_of(me_ctx * cols, cols), cols)
    outs = ((layer, layer_out), (first, first_out), (second, second_out))
    for which, (src, dst) in enumerate(((terms, terms_in),) + outs):
        group = copies.setdefault(which, [])
        for step in range(1, ctx):
            peer = lax.rem(me_ctx + step, ctx)
            group.append(
                send(
                    src.at[pl.ds(pl.multiple_of(peer * rows, rows), rows)],
                    dst.at[me_ctx] if which == 0 else dst.at[:, mine],
                    ctx_send.at[which, step], ctx_recv.at[which, step], (me_dp, peer),
                )
            )
        part = src.at[pl.ds(pl.multiple_of(me_ctx * rows, rows), rows)]
        group.append(
            pltpu.make_async_copy(
                part, dst.at[me_ctx] if which == 0 else dst.at[:, mine], local_sem.at[which]
            )
        )
    group = copies.setdefault(4, [])
    for kind, (src, dst) in enumerate(((short_send, short_in), (medium_send, medium_in))):
        for step in range(1, dp):
            peer = lax.rem(me_dp + step, dp)
            group.append(
                send(
                    src, dst.at[me_dp], small_send.at[kind, step], small_recv.at[kind, step],
                    (peer, me_ctx),
                )
            )
        group.append(pltpu.make_async_copy(src, dst.at[me_dp], local_sem.at[4 + kind]))
    for copy in copies[0]:
        copy.start()

    steps = layer.shape[1] // LANES
    groups = LANES // group_width
    clear(scratch, layer.shape[0], scratch[6].shape[1] // 2)
    short[...] = jnp.zeros_like(short)

    def mixer_step(step, carry):
        lanes, owned = lane_block(step), group_rows(step, groups)
        mixer_block(
            group_width, gate_in.at[:, lanes], gate_out.at[:, lanes], values.at[:, lanes],
            cot.at[:, lanes], taps.at[:, :, lanes], ahead.at[owned], behind.at[owned],
            layer.at[:, lanes], first.at[:, lanes], second.at[:, lanes], short.at[:, lanes],
            medium.at[owned], scratch,
        )
        return carry

    span = 32

    def add(spot, source):
        def body(step, carry):
            part = pl.ds(pl.multiple_of(step * span, span), span)
            held[spot, part] = (
                held[spot, part].astype(jnp.float32) + source[spot, part].astype(jnp.float32)
            ).astype(jnp.bfloat16)
            return carry

        lax.fori_loop(0, depth // span, body, 0)

    def ready(spot):
        keep(spot).wait()
        if pair == 2:
            swap(spot).wait_recv()
            add(spot, from_pair)

    def go_right(spot):
        ready(spot)

        @pl.when(at > 0)
        def _():
            to_right(spot).wait_recv()
            add(spot, from_left)

        to_right(spot).start()

    def go_left(spot):
        ready(spot)

        @pl.when(at + 1 < line)
        def _():
            to_left(spot).wait_recv()
            add(spot, from_right)

        to_left(spot).start()

    early = steps * 5 // 8
    lax.fori_loop(0, early, mixer_step, 0)
    for far in range(line - 1, 0, -1):
        pl.when(at + far < line)(functools.partial(go_right, at + far))
        pl.when(at - far >= 0)(functools.partial(go_left, at - far))
        if far == line - 1:
            lax.fori_loop(early, steps, mixer_step, 0)
            short_send[...] = (short[...] * row_scale).astype(BF16)
            medium_send[...] = (medium[...] * group_scale).astype(BF16)
            for which in (1, 2, 3, 4):
                for copy in copies[which]:
                    copy.start()
    for copy in copies[0]:
        copy.wait()

    def sum_terms(step, carry):
        part = pl.ds(pl.multiple_of(step * 16, 16), 16)
        summed = terms_in[0, part].astype(F32)
        for peer in range(1, ctx):
            summed = summed + terms_in[peer, part].astype(F32)
        features_out[part] = summed.astype(BF16)
        return carry

    lax.fori_loop(0, rows // 16, sum_terms, 0)
    for copy in copies[4]:
        copy.wait()
    summed = short_in[0].astype(F32)
    whole = medium_in[0].astype(F32)
    for peer in range(1, dp):
        summed = summed + short_in[peer].astype(F32)
        whole = whole + medium_in[peer].astype(F32)
    edge = short_out.shape[1]
    for index in range(3):
        short_out[index] = summed[8 * index : 8 * index + edge]
    medium_out[...] = whole
    ready(at)

    @pl.when(at > 0)
    def _():
        to_right(at).wait_recv()
        add(at, from_left)

    @pl.when(at + 1 < line)
    def _():
        to_left(at).wait_recv()
        add(at, from_right)

    result = pltpu.make_async_copy(held.at[at], weight_out, out_sem)
    result.start()
    for which in (1, 2, 3):
        for copy in copies[which]:
            copy.wait()
    for spot in range(line):
        if pair == 2:
            swap(spot).wait_send()
        pl.when(spot > at)(lambda spot=spot: to_right(spot).wait_send())
        pl.when(spot < at)(lambda spot=spot: to_left(spot).wait_send())
    result.wait()


def scatter_all(
    dp, ctx, group_width, row_scale, group_scale,
    grad_weight, terms, gate_in, gate_out, values, cot, taps, ahead, behind,
):
    pair = 2 if dp % 2 == 0 else 1
    line = dp // pair
    length, cols = values.shape
    edge, span = taps.shape[1], ahead.shape[1] // 2
    group_count = ahead.shape[0]
    rows, channels, depth = length // ctx, terms.shape[1], grad_weight.shape[0] // dp
    shapes = [(depth, cols)] + [(rows, channels)] * 4
    dma = pltpu.SemaphoreType.DMA
    slots = pltpu.VMEM((line, depth, cols), BF16)
    block = pltpu.VMEM((length, cols), BF16)
    return pl.pallas_call(
        functools.partial(scatter_kernel, dp, ctx, pair, group_width, row_scale, group_scale),
        out_shape=[jax.ShapeDtypeStruct(shape, BF16) for shape in shapes]
        + [
            jax.ShapeDtypeStruct((3, edge, cols), F32),
            jax.ShapeDtypeStruct((group_count, span), F32),
        ],
        in_specs=[ANY] * 2 + [VMEM] * 7,
        out_specs=[ANY, VMEM] + [ANY] * 3 + [VMEM] * 2,
        scratch_shapes=[slots] * 4
        + [
            pltpu.VMEM((ctx, rows, channels), BF16), block, block, block,
            pltpu.VMEM((32, cols), F32), pltpu.VMEM((group_count, span), F32),
            pltpu.VMEM((32, cols), BF16), pltpu.VMEM((group_count, span), BF16),
            pltpu.VMEM((dp, 32, cols), BF16), pltpu.VMEM((dp, group_count, span), BF16),
        ]
        + [dma((6,)), dma((line,)), dma((4, ctx)), dma((4, ctx)), dma((2, dp)), dma((2, dp))]
        + [dma((line,))] * 6
        + [dma]
        + mixer_scratch(length, span, group_width),
        compiler_params=pltpu.CompilerParams(
            collective_id=1, has_side_effects=True, vmem_limit_bytes=50 * 2**20
        ),
    )(grad_weight, terms, gate_in, gate_out, values, cot, taps, ahead, behind)


def local(features, gate_in, gate_out, value_weight, short_taps, medium_taps, cotangent):
    ctx = lax.axis_size("ctx")
    dp = lax.axis_size("dp")
    ctx_index = lax.axis_index("ctx")
    rows, channels = features.shape
    cols = value_weight.shape[1]
    span, group_count = medium_taps.shape
    group_width = channels // group_count
    total_rows = rows * ctx * dp
    row_scale = 1.0 / math.sqrt(total_rows)
    group_scale = 1.0 / math.sqrt(total_rows * group_width)
    taps = lax.dynamic_slice_in_dim(short_taps, ctx_index * cols, cols, 2)
    own_groups = group_count // ctx
    medium = lax.dynamic_slice_in_dim(medium_taps, ctx_index * own_groups, own_groups, 1)
    lifted = medium.astype(F32).T
    zeros = jnp.zeros((own_groups, span), F32)
    ahead = jnp.concatenate([zeros[:, :1], lifted[:, ::-1], zeros[:, 1:]], axis=1)
    behind = jnp.concatenate([lifted, zeros], axis=1)
    window, block_in, block_out, block_cot, values, grad_values, terms = gather_all(
        dp, ctx, group_width, features, gate_in, gate_out, cotangent, value_weight, taps, behind
    )
    grad_weight = (
        lax.dot_general(window, grad_values, (((0,), (0,)), ((), ())), preferred_element_type=F32)
        * row_scale
    ).astype(BF16)
    weight_out, grad_features, layer_out, first_out, second_out, grad_short, grad_medium = (
        scatter_all(
            dp, ctx, group_width, row_scale, group_scale,
            grad_weight, terms, block_in, block_out, values, block_cot, taps, ahead, behind,
        )
    )
    return (
        layer_out,
        grad_features,
        first_out,
        second_out,
        weight_out,
        grad_short,
        grad_medium[:, ::-1].T,
    )


def solution(mesh):
    rows, split = P(("dp", "ctx"), None), P("dp", "ctx")
    return jax.shard_map(
        local,
        mesh=mesh,
        in_specs=(rows, rows, rows, split, P(), P(), rows),
        out_specs=(rows, rows, rows, rows, split, P(None, None, "ctx"), P(None, "ctx")),
        check_vma=False,
    )
```

time: 285 us -> 239 us (0.84)
  Pallas kernels: 236 us -> 211 us
  matrix products: 24.6 us -> 10.3 us
  other arithmetic: 4.43 us -> 0.1 us
  local copies, waits for them, and re-layouts: 19.1 us -> 14.9 us
    pallas_call x3 -> x2, Pallas kernels: 236 us -> 211 us  [the longest x1 106 us: scatter_all(): pl.pallas_call(functools.partial(scatter_kernel, dp, ctx, pair, group_wid...]
    dot_general x2 -> x0, matrix products: 15.4 us -> none  [the longest x1 9.28 us: local(): values = jnp.dot(window, weight, preferred_element_type=f32).astype(bf16)]
    reduce_sum x2 -> x0, other arithmetic: 4.3 us -> none  [the longest x1 4.22 us: local(): grad_features = jnp.sum(terms_out.astype(f32), axis=0).astype(bf16)]
    reshape x5 -> x0, local copies, waits for them, and re-layouts: 3.84 us -> none  [the longest x1 1.54 us: local(): sums[:short_size].reshape(grad_short.shape)]
    unnamed x34 -> x21, local copies, waits for them, and re-layouts: 12.7 us -> 12.4 us
where the time goes in v2:
time: 239 us; the launch traced here: 237 us
  Pallas kernels  211 us (88%)
  local copies, waits for them, and re-layouts  14.9 us (6%)
  matrix products  10.3 us (4%)
    pallas_call x1, Pallas kernels, scatter_all(): pl.pallas_call(functools.partial(scatter_kernel, dp, ctx, pair, group_wid...  106 us
    pallas_call x1, Pallas kernels, gather_all(): pl.pallas_call(functools.partial(gather_kernel, dp, ctx, pair, group_widt...  105 us
    unnamed x21, local copies, waits for them, and re-layouts  12.4 us
    dot_general x1, matrix products, local(): lax.dot_general(window, grad_values, (((0,), (0,)), ((), ())), preferred_...  10.3 us

profile of v2, /device:TPU:0, one launch (start us, length us, event | category | flops | bytes accessed | tf_op | source)
XLA Modules:
  0.0 237.0 jit_solution(15601246738643851425)
XLA Ops:
  0.6 0.0 copy-start
  0.7 0.1 pad.3.clone
  0.7 0.9 constant_dynamic-slice_fusion
  1.6 0.1 copy.15
  1.7 0.1 rev.6
  1.8 0.1 maximum_maximum_fusion.ahead
  1.9 104.6 %shard_map.126 = (bf16[512,4096]{1,0:T(8,128)(2,1)}, bf16[512,1024]{1,0:T(8,128)(2,1)S(1)}, bf16[512,1024]{1,0:T(8,128)(2,1)S(1)}, bf16[512,1024]{1,0:T(8,128)(2...) custom-call(bf16[128,4096]{1,0:T(8,128)(2,1)} %features.1, ...), custom_call_target="tpu_custom_call" | custom-call | tf_op jit(solution)/shard_map/pallas_call | solution.py:381
  106.6 0.0 copy-start.1
  106.6 1.0 copy-done.1
  107.5 1.0 copy-done.2
  108.5 1.0 copy-done.3
  109.5 10.3 %multiply_convert_fusion.grad_weight = bf16[4096,1024]{1,0:T(8,128)(2,1)} fusion(bf16[512,4096]{1,0:T(8,128)(2,1)} %get-tuple-element.21, bf16[512,1024]{1,0:T(8,128)(2,1)} %get-tuple-element.22), kind=kOutput, calls=%fused_computation | convolution fusion | flops 4303355904 | bytes 13631488 | tf_op jit(solution)/shard_map/dot_general | solution.py:660
  119.8 106.4 %shard_map.127 = (bf16[512,1024]{1,0:T(8,128)(2,1)S(1)}, bf16[128,4096]{1,0:T(8,128)(2,1)S(1)}, bf16[128,4096]{1,0:T(8,128)(2,1)S(1)}, bf16[128,4096]{1,0:T(8,12...) custom-call(bf16[4096,1024]{1,0:T(8,128)(2,1)} %multiply_convert_fusion.grad_weight, ...), custom_call_target="tpu_custom_call" | custom-call | tf_op jit(solution)/shard_map/pallas_call | solution.py:612
  226.2 0.0 copy-start.4
  226.2 0.6 copy-done.4
  226.9 0.6 copy-done.6
  227.5 1.4 rev.7
  228.9 1.0 copy.22
  229.9 1.0 copy.23
  230.9 2.3 copy.24
  233.1 2.3 copy.25
  235.4 1.0 copy.26
  236.4 0.0 copy-done.5
  236.4 0.6 copy.27
  (10 shorter events, 0.0 us)
Async XLA Ops:
  0.6 1.3 copy-start
  106.6 1.0 copy-start.1
  107.5 1.0 copy-start.2
  108.5 1.0 copy-start.3
  226.2 0.6 copy-start.4
  226.9 0.6 copy-start.6
  228.9 7.5 %copy-start.5 = (f32[3,7,1024]{2,1,0:T(8,128)S(1)}, f32[3,7,1024]{2,1,0:T(8,128)}, u32[]{:S(2)}) copy-start(f32[3,7,1024]{2,1,0:T(8,128)} %copy-done.4) | copy-start | bytes 258052

commit v3 on v2

--- a/solution.py
+++ b/solution.py
@@ -201,6 +201,7 @@
     window_out, in_out, out_out, cot_out, values, grad_values, terms,
     window, block_in, block_out, block_cot, full, total,
     local_sem, ctx_send, ctx_recv, right_send, left_send, pair_send, full_recv, out_sem,
+    half_send, half_recv,
     *scratch,
 ):
     me_dp, me_ctx = lax.axis_index("dp"), lax.axis_index("ctx")
@@ -216,9 +217,30 @@
     def push(src, index, sem, to):
         return send(src, block(index), sem, full_recv.at[index], (to, me_ctx))
 
+    halves = pair == 2 and line % 2 == 0
+    buddy = at + 1 - 2 * lax.rem(at, 2)
+    half = depth // 2
+
+    def across(index, src):
+        return push(src, index, pair_send.at[index // pair], at * pair + 1 - side)
+
+    def across_half(index):
+        top = full.at[index, pl.ds(0, half)]
+        return send(
+            top, top, pair_send.at[index // pair], full_recv.at[index],
+            (at * pair + 1 - side, me_ctx),
+        )
+
+    def along_half():
+        low = full.at[at * pair + 1 - side, pl.ds(half, half)]
+        return send(low, low, half_send, half_recv, (buddy * pair + side, me_ctx))
+
     def others(index, src):
-        if pair == 2:
-            push(src, index, pair_send.at[index // pair], at * pair + 1 - side).start()
+        if halves:
+            pl.when(index // pair == buddy)(lambda: across_half(index).start())
+            pl.when(index // pair != buddy)(lambda: across(index, src).start())
+        elif pair == 2:
+            across(index, src).start()
 
     @pl.when(at + 1 < line)
     def _():
@@ -307,6 +329,10 @@
 
     if line > 1:
         relay(1)
+    if pair == 2:
+        arrived(at * pair + 1 - side)
+    if halves:
+        along_half().start()
     for which in (1, 2, 3):
         for copy in copies[which]:
             copy.wait()
@@ -339,8 +365,18 @@
         return carry
 
     def far_both(step, carry):
-        index = lax.rem(at + step, line) * pair + 1 - side
-        arrived(index)
+        spot = lax.rem(at + step, line)
+        index = spot * pair + 1 - side
+        if halves:
+            @pl.when(spot == buddy)
+            def _():
+                across_half(index).wait_recv()
+                low = full.at[index, pl.ds(half, half)]
+                send(low, low, half_send, half_recv, (buddy * pair + side, me_ctx)).wait_recv()
+
+            pl.when((step > 0) & (spot != buddy))(lambda: arrived(index))
+        else:
+            pl.when(step > 0)(lambda: arrived(index))
         add_terms(index)
         add_values(index)
         return carry
@@ -352,12 +388,19 @@
     lax.fori_loop(0, line, near_values, 0)
     if pair == 2:
         lax.fori_loop(0, line, far_both, 0)
+    if halves:
+        along_half().wait_send()
     values[...] = total[...].astype(BF16)
     for leave in leaves:
         leave.wait()
     for spot in range(line):
-        if pair == 2:
-            push(weight, me_dp, pair_send.at[spot], me_dp).wait_send()
+        if halves:
+            pl.when(spot == buddy)(lambda spot=spot: across_half(spot * pair + side).wait_send())
+            pl.when(spot != buddy)(
+                lambda spot=spot: across(spot * pair + side, weight).wait_send()
+            )
+        elif pair == 2:
+            across(spot * pair + side, weight).wait_send()
 
         @pl.when((at + 1 < line) & (spot <= at))
         def _():
@@ -387,7 +430,7 @@
             pltpu.VMEM((length, channels), BF16), block, block, block,
             pltpu.VMEM((dp, depth, cols), BF16), pltpu.VMEM((length, cols), F32),
             dma((5,)), dma((4, ctx)), dma((4, ctx)), dma((line,)), dma((line,)), dma((line,)),
-            dma((dp,)), dma((4,)),
+            dma((dp,)), dma((4,)), dma, dma,
         ]
         + mixer_scratch(length, span, group_width),
         compiler_params=pltpu.CompilerParams(
@@ -399,11 +442,11 @@
 def scatter_kernel(
     dp, ctx, pair,
     group_width, row_scale, group_scale,
-    grad_weight, terms, gate_in, gate_out, values, cot, taps, ahead, behind,
+    window, grad_values, terms, gate_in, gate_out, values, cot, taps, ahead, behind,
     weight_out, features_out, layer_out, first_out, second_out, short_out, medium_out,
-    held, from_pair, from_left, from_right,
+    held, from_pair, from_left, from_right, outgoing, from_buddy,
     terms_in, layer, first, second, short, medium, short_send, medium_send, short_in, medium_in,
-    local_sem, held_sem, ctx_send, ctx_recv, small_send, small_recv,
+    local_sem, buddy_send, buddy_recv, ctx_send, ctx_recv, small_send, small_recv,
     pair_send, pair_recv, right_send, left_recv, left_send, right_recv, out_sem,
     *scratch,
 ):
@@ -414,15 +457,36 @@
     depth = weight_out.shape[0]
     greet(dp, ctx)
 
-    def block(index):
-        return grad_weight.at[pl.ds(pl.multiple_of(index * depth, depth), depth)]
-
-    def keep(spot):
-        return pltpu.make_async_copy(block(spot * pair + side), held.at[spot], held_sem.at[spot])
+    halves = pair == 2 and line % 2 == 0
+    buddy = at + 1 - 2 * lax.rem(at, 2)
+    half = depth // 2
+
+    def make(index, target, spot):
+        part = pl.ds(pl.multiple_of(index * depth, depth), depth)
+        target[spot] = (
+            lax.dot_general(
+                window[:, part], grad_values[...], (((0,), (0,)), ((), ())),
+                preferred_element_type=F32,
+            )
+            * row_scale
+        ).astype(BF16)
+
+    def swap_half(spot):
+        top = pl.ds(0, half)
+        return send(
+            outgoing.at[spot, top], from_pair.at[spot, top], pair_send.at[spot],
+            pair_recv.at[spot], (at * pair + 1 - side, me_ctx),
+        )
+
+    def to_buddy():
+        return send(
+            outgoing.at[buddy, pl.ds(half, half)], from_buddy, buddy_send, buddy_recv,
+            (buddy * pair + side, me_ctx),
+        )
 
     def swap(spot):
         return send(
-            block(spot * pair + 1 - side), from_pair.at[spot], pair_send.at[spot],
+            outgoing.at[spot], from_pair.at[spot], pair_send.at[spot],
             pair_recv.at[spot], (at * pair + 1 - side, me_ctx),
         )
 
@@ -437,16 +501,6 @@
             held.at[spot], from_right.at[spot], left_send.at[spot], right_recv.at[spot],
             (me_dp - pair, me_ctx),
         )
-
-    def begin(spot):
-        if pair == 2:
-            swap(spot).start()
-        keep(spot).start()
-
-    for far in range(line - 1, 0, -1):
-        pl.when(at + far < line)(functools.partial(begin, at + far))
-        pl.when(at - far >= 0)(functools.partial(begin, at - far))
-    begin(at)
 
     copies = {}
     mine = pl.ds(pl.multiple_of(me_ctx * cols, cols), cols)
@@ -481,7 +535,43 @@
         group.append(pltpu.make_async_copy(src, dst.at[me_dp], local_sem.at[4 + kind]))
     for copy in copies[0]:
         copy.start()
-
+    span = 32
+
+    def begin(step, carry):
+        spot = at + (1 - 2 * lax.rem(step, 2)) * (line - 1 - step // 2)
+
+        @pl.when((spot >= 0) & (spot < line))
+        def _():
+            if pair == 2:
+                make(spot * pair + 1 - side, outgoing, spot)
+            if halves:
+                @pl.when(spot == buddy)
+                def _():
+                    swap_half(spot).start()
+                    to_buddy().start()
+
+                @pl.when(spot == at)
+                def _():
+                    to_buddy().wait_recv()
+
+                    def join(row, carry):
+                        part = pl.ds(pl.multiple_of(row * span, span), span)
+                        low = pl.ds(pl.multiple_of(half + row * span, span), span)
+                        outgoing[at, low] = (
+                            outgoing[at, low].astype(F32) + from_buddy[part].astype(F32)
+                        ).astype(BF16)
+                        return carry
+
+                    lax.fori_loop(0, half // span, join, 0)
+
+                pl.when(spot != buddy)(lambda: swap(spot).start())
+            elif pair == 2:
+                swap(spot).start()
+            make(spot * pair + side, held, spot)
+
+        return carry
+
+    lax.fori_loop(0, 2 * line - 1, begin, 0)
     steps = layer.shape[1] // LANES
     groups = LANES // group_width
     clear(scratch, layer.shape[0], scratch[6].shape[1] // 2)
@@ -497,9 +587,7 @@
         )
         return carry
 
-    span = 32
-
-    def add(spot, source):
+    def add(spot, source, count=depth):
         def body(step, carry):
             part = pl.ds(pl.multiple_of(step * span, span), span)
             held[spot, part] = (
@@ -507,13 +595,22 @@
             ).astype(jnp.bfloat16)
             return carry
 
-        lax.fori_loop(0, depth // span, body, 0)
+        lax.fori_loop(0, count // span, body, 0)
 
     def ready(spot):
-        keep(spot).wait()
-        if pair == 2:
+        def whole():
             swap(spot).wait_recv()
             add(spot, from_pair)
+
+        def part():
+            swap_half(spot).wait_recv()
+            add(spot, from_pair, half)
+
+        if halves:
+            pl.when(spot == buddy)(part)
+            pl.when(spot != buddy)(whole)
+        elif pair == 2:
+            whole()
 
     def go_right(spot):
         ready(spot)
@@ -535,7 +632,7 @@
 
         to_left(spot).start()
 
-    early = steps * 5 // 8
+    early = steps * 3 // 8
     lax.fori_loop(0, early, mixer_step, 0)
     for far in range(line - 1, 0, -1):
         pl.when(at + far < line)(functools.partial(go_right, at + far))
@@ -588,23 +685,28 @@
         for copy in copies[which]:
             copy.wait()
     for spot in range(line):
-        if pair == 2:
+        if halves:
+            pl.when(spot == buddy)(lambda spot=spot: swap_half(spot).wait_send())
+            pl.when(spot != buddy)(lambda spot=spot: swap(spot).wait_send())
+        elif pair == 2:
             swap(spot).wait_send()
         pl.when(spot > at)(lambda spot=spot: to_right(spot).wait_send())
         pl.when(spot < at)(lambda spot=spot: to_left(spot).wait_send())
+    if halves:
+        to_buddy().wait_send()
     result.wait()
 
 
 def scatter_all(
     dp, ctx, group_width, row_scale, group_scale,
-    grad_weight, terms, gate_in, gate_out, values, cot, taps, ahead, behind,
+    window, grad_values, terms, gate_in, gate_out, values, cot, taps, ahead, behind,
 ):
     pair = 2 if dp % 2 == 0 else 1
     line = dp // pair
     length, cols = values.shape
     edge, span = taps.shape[1], ahead.shape[1] // 2
     group_count = ahead.shape[0]
-    rows, channels, depth = length // ctx, terms.shape[1], grad_weight.shape[0] // dp
+    rows, channels, depth = length // ctx, terms.shape[1], window.shape[1] // dp
     shapes = [(depth, cols)] + [(rows, channels)] * 4
     dma = pltpu.SemaphoreType.DMA
     slots = pltpu.VMEM((line, depth, cols), BF16)
@@ -616,23 +718,24 @@
             jax.ShapeDtypeStruct((3, edge, cols), F32),
             jax.ShapeDtypeStruct((group_count, span), F32),
         ],
-        in_specs=[ANY] * 2 + [VMEM] * 7,
+        in_specs=[VMEM] * 2 + [ANY] + [VMEM] * 7,
         out_specs=[ANY, VMEM] + [ANY] * 3 + [VMEM] * 2,
-        scratch_shapes=[slots] * 4
+        scratch_shapes=[slots] * 5
+        + [pltpu.VMEM((depth // 2, cols), BF16)]
         + [
             pltpu.VMEM((ctx, rows, channels), BF16), block, block, block,
             pltpu.VMEM((32, cols), F32), pltpu.VMEM((group_count, span), F32),
             pltpu.VMEM((32, cols), BF16), pltpu.VMEM((group_count, span), BF16),
             pltpu.VMEM((dp, 32, cols), BF16), pltpu.VMEM((dp, group_count, span), BF16),
         ]
-        + [dma((6,)), dma((line,)), dma((4, ctx)), dma((4, ctx)), dma((2, dp)), dma((2, dp))]
+        + [dma((6,)), dma, dma, dma((4, ctx)), dma((4, ctx)), dma((2, dp)), dma((2, dp))]
         + [dma((line,))] * 6
         + [dma]
         + mixer_scratch(length, span, group_width),
         compiler_params=pltpu.CompilerParams(
             collective_id=1, has_side_effects=True, vmem_limit_bytes=50 * 2**20
         ),
-    )(grad_weight, terms, gate_in, gate_out, values, cot, taps, ahead, behind)
+    )(window, grad_values, terms, gate_in, gate_out, values, cot, taps, ahead, behind)
 
 
 def local(features, gate_in, gate_out, value_weight, short_taps, medium_taps, cotangent):
@@ -656,14 +759,10 @@
     window, block_in, block_out, block_cot, values, grad_values, terms = gather_all(
         dp, ctx, group_width, features, gate_in, gate_out, cotangent, value_weight, taps, behind
     )
-    grad_weight = (
-        lax.dot_general(window, grad_values, (((0,), (0,)), ((), ())), preferred_element_type=F32)
-        * row_scale
-    ).astype(BF16)
     weight_out, grad_features, layer_out, first_out, second_out, grad_short, grad_medium = (
         scatter_all(
             dp, ctx, group_width, row_scale, group_scale,
-            grad_weight, terms, block_in, block_out, values, block_cot, taps, ahead, behind,
+            window, grad_values, terms, block_in, block_out, values, block_cot, taps, ahead, behind,
         )
     )
     return (

time: 239 us -> 247 us (1.033)
  Pallas kernels: 211 us -> 233 us
  matrix products: 10.3 us -> 0 us
  local copies, waits for them, and re-layouts: 14.9 us -> 12.2 us
    pallas_call x1, Pallas kernels: 106 us -> 118 us  [scatter_all(): pl.pallas_call(functools.partial(scatter_kernel, dp, ctx, pair, group_wid...]
    dot_general x1 -> x0, matrix products: 10.3 us -> none  [local(): lax.dot_general(window, grad_values, (((0,), (0,)), ((), ())), preferred_...]
    pallas_call x1, Pallas kernels: 105 us -> 115 us  [gather_all(): pl.pallas_call(functools.partial(gather_kernel, dp, ctx, pair, group_widt...]
    unnamed x21 -> x25, local copies, waits for them, and re-layouts: 12.4 us -> 9.75 us
where the time goes in v3:
time: 247 us; the launch traced here: 246 us
  Pallas kernels  233 us (94%)
  local copies, waits for them, and re-layouts  12.2 us (5%)
    pallas_call x1, Pallas kernels, scatter_all(): pl.pallas_call(functools.partial(scatter_kernel, dp, ctx, pair, group_wid...  118 us
    pallas_call x1, Pallas kernels, gather_all(): pl.pallas_call(functools.partial(gather_kernel, dp, ctx, pair, group_widt...  115 us
    unnamed x25, local copies, waits for them, and re-layouts  9.75 us

profile of v3, /device:TPU:0, one launch (start us, length us, event | category | flops | bytes accessed | tf_op | source)
XLA Modules:
  0.0 246.3 jit_solution(9801862087390388159)
XLA Ops:
  0.6 0.0 copy-start
  0.7 0.1 pad.3.clone
  0.7 0.9 constant_dynamic-slice_fusion
  1.6 0.1 copy.15
  1.7 0.1 rev.6
  1.8 0.1 maximum_maximum_fusion.ahead
  1.9 0.0 copy-done
  1.9 114.8 %shard_map.126 = (bf16[512,4096]{1,0:T(8,128)(2,1)}, bf16[512,1024]{1,0:T(8,128)(2,1)S(1)}, bf16[512,1024]{1,0:T(8,128)(2,1)S(1)}, bf16[512,1024]{1,0:T(8,128)(2...) custom-call(bf16[128,4096]{1,0:T(8,128)(2,1)} %features.1, ...), custom_call_target="tpu_custom_call" | custom-call | tf_op jit(solution)/shard_map/pallas_call | solution.py:424
  116.7 0.0 copy-start.1
  116.8 1.0 copy-done.1
  117.7 1.0 copy-done.2
  118.7 1.0 copy-done.3
  119.7 118.5 %shard_map.127 = (bf16[512,1024]{1,0:T(8,128)(2,1)S(1)}, bf16[128,4096]{1,0:T(8,128)(2,1)S(1)}, bf16[128,4096]{1,0:T(8,128)(2,1)S(1)}, bf16[128,4096]{1,0:T(8,12...) custom-call(bf16[512,4096]{1,0:T(8,128)(2,1)} %get-tuple-element.21.window, ...), custom_call_target="tpu_custom_call" | custom-call | tf_op jit(solution)/shard_map/pallas_call | solution.py:714
  238.1 0.0 copy-start.4
  238.1 0.6 copy-done.4
  238.8 0.6 copy-done.6
  239.4 1.4 rev.7
  240.8 1.0 copy.22
  241.8 1.0 copy.23
  242.8 1.0 copy.24
  243.7 1.0 copy.25
  244.7 1.0 copy.26
  245.7 0.0 copy-done.5
  245.7 0.6 copy.27
  (13 shorter events, 0.0 us)
Async XLA Ops:
  0.6 1.3 copy-start
  116.7 1.0 copy-start.1
  117.7 1.0 copy-start.2
  118.7 1.0 copy-start.3
  238.1 0.6 copy-start.4
  238.8 0.6 copy-start.6
  240.8 1.9 copy-start.8
  240.8 2.9 %copy-start.7 = (bf16[128,4096]{1,0:T(8,128)(2,1)S(1)}, bf16[128,4096]{1,0:T(8,128)(2,1)}, u32[]{:S(2)}) copy-start(bf16[128,4096]{1,0:T(8,128)(2,1)} %get-tuple-element.45) | copy-start | bytes 3145732
  241.8 3.9 %copy-start.5 = (f32[3,7,1024]{2,1,0:T(8,128)S(1)}, f32[3,7,1024]{2,1,0:T(8,128)}, u32[]{:S(2)}) copy-start(f32[3,7,1024]{2,1,0:T(8,128)} %copy-done.4) | copy-start | bytes 258052
